TPU v7x, 128 devices: a whole 4x4x4 slice. The times are simulated.
128 devices in a mesh: dp: 4 (over z), seq: 32 (over x, y, core).
Axes of the slice: x: 4, y: 4, z: 4, core: 2. Of those that a mesh axis runs over, the one named last changes fastest.
Arguments:
- mixed: bfloat16 [4, 4096, 4096], P('dp', 'seq'), may hold values from -6 to 6
- conv_weight: bfloat16 [4, 4096], replicated, may hold values from -3 to 3
- log_decay: float32 [4, 16, 4096], P('dp', None, 'seq'), may hold values from -0.75 to 0, as said below
- beta: float32 [4, 16, 4096], P('dp', None, 'seq'), may hold values from 0.01 to 0.5
- doc_ids: int32 [4, 4096], P('dp', 'seq'), may hold values from 0 to 7, never falling along the last dimension, each value on 1 to 1024 neighbouring positions
- out_grad: bfloat16 [4, 4096, 2048], P('dp', 'seq'), may hold values from -6 to 6
Outputs:
- output: bfloat16 [4, 4096, 2048], P('dp', 'seq')
- d_mixed: bfloat16 [4, 4096, 4096], P('dp', 'seq')
- d_conv_weight: float32 [4, 4096], replicated
- d_log_decay: float32 [4, 16, 4096], P('dp', None, 'seq')
- d_beta: float32 [4, 16, 4096], P('dp', None, 'seq')
Inputs may be any that keep to these rules, and one draw needn't show every extreme that they name: `doc_ids`: document numbers never fall along a slab; each of the 8 documents holds 1 to 1024 tokens, and one holds exactly 1024. `log_decay`: every entry is negative.
All inputs are finite; a program needn't handle non-finite values.
Results may differ from a plain program's by a relative error of at most 0.00115.
Values may be sent and summed in bfloat16 or wider, within the bound.
A program may use at most 128 MiB of HBM per device.

v0:
```python
import jax
import jax.numpy as jnp
from jax import lax
from jax.sharding import PartitionSpec as P

DK = 128
KH = 8
VH = 16
CH = 64
SPAN = 8


highest_precision = lax.Precision.HIGHEST
epsilon = 1e-06


def passed_along(array, axis, by):
    length = lax.axis_size(axis)
    pairs = [(i, i + by) for i in range(length) if 0 <= i + by < length]
    return lax.ppermute(array, axis, pairs)


def unit_norm(values):
    return values * lax.rsqrt(jnp.sum(values * values, -1, keepdims=True) + epsilon)


def compose(earlier, later):
    first_map, first_shift = earlier
    second_map, second_shift = later
    joined = jnp.einsum("hij,hjk->hik", second_map, first_map, precision=highest_precision)
    moved = (
        jnp.einsum("hij,hjk->hik", second_map, first_shift, precision=highest_precision)
        + second_shift
    )
    return (joined, moved)


def advance(transition, offset_term, carried):
    return (
        jnp.einsum("hij,hjk->hik", transition, carried, precision=highest_precision) + offset_term
    )


def prepare(rows_ext, weight, decay, rate, docs_ext, key_heads, per_key, value_width):
    length = rows_ext.shape[0] - 3
    head_count = decay.shape[0]
    own_docs = docs_ext[3:]
    summed = weight[3] * rows_ext[3:]
    for offset in (1, 2, 3):
        earlier_docs = docs_ext[3 - offset : 3 - offset + length]
        earlier_rows = rows_ext[3 - offset : 3 - offset + length]
        summed = summed + weight[3 - offset] * jnp.where(
            (earlier_docs == own_docs)[:, None], earlier_rows, 0.0
        )
    active = jax.nn.silu(summed)
    query_matrix = active[:, : key_heads * DK].reshape(length, key_heads, DK)
    key_rows = active[:, key_heads * DK : 2 * key_heads * DK].reshape(length, key_heads, DK)
    values = active[:, 2 * key_heads * DK :].reshape(length, head_count, value_width)
    query_matrix = jnp.repeat(unit_norm(query_matrix) * DK ** (-0.5), per_key, axis=1)
    key_rows = jnp.repeat(unit_norm(key_rows), per_key, axis=1)
    blocks = length // CH

    def split_blocks(array):
        return array.reshape(blocks, CH, head_count, -1).transpose(0, 2, 1, 3)

    query_blocks = split_blocks(query_matrix)
    key_blocks = split_blocks(key_rows)
    value_blocks = split_blocks(values)
    cumulated = jnp.cumsum(decay.reshape(head_count, blocks, CH).transpose(1, 0, 2), axis=-1)
    rate_blocks = rate.reshape(head_count, blocks, CH).transpose(1, 0, 2)
    doc_blocks = own_docs.reshape(blocks, CH)
    before = docs_ext[2 : 2 + length].reshape(blocks, CH)[:, 0]
    carry_in = (doc_blocks == before[:, None]).astype(jnp.float32)
    positions = jnp.arange(CH)
    lower = positions[:, None] >= positions[None, :]
    strict = positions[:, None] > positions[None, :]
    same_doc = doc_blocks[:, :, None] == doc_blocks[:, None, :]
    gaps = cumulated[..., :, None] - cumulated[..., None, :]
    fading = jnp.where((same_doc & lower)[:, None], jnp.exp(jnp.minimum(gaps, 0.0)), 0.0)
    key_inner = jnp.einsum("nhik,nhjk->nhij", key_blocks, key_blocks, precision=highest_precision)
    triangle = jnp.eye(CH, dtype=jnp.float32) + jnp.where(
        strict, rate_blocks[..., :, None] * key_inner * fading, 0.0
    )
    entry_scale = carry_in[:, None, :] * jnp.exp(cumulated)
    right_side = jnp.concatenate(
        [
            (rate_blocks * entry_scale)[..., None] * key_blocks,
            rate_blocks[..., None] * value_blocks,
        ],
        -1,
    )
    solved = jax.scipy.linalg.solve_triangular(triangle, right_side, lower=True, unit_diagonal=True)
    woodbury_keys = solved[..., :DK]
    woodbury_values = solved[..., DK:]
    scores = (
        jnp.einsum("nhik,nhjk->nhij", query_blocks, key_blocks, precision=highest_precision)
        * fading
    )
    query_entering = entry_scale[..., None] * query_blocks
    tail = jnp.where(
        (doc_blocks == doc_blocks[:, -1:])[:, None, :],
        jnp.exp(cumulated[..., -1:] - cumulated),
        0.0,
    )
    key_result = tail[..., None] * key_blocks
    keep_last = carry_in[:, None, -1] * jnp.exp(cumulated[..., -1])
    return (query_entering, scores, woodbury_keys, woodbury_values, key_result, keep_last)


def chain_terms(parts):
    query_entering, scores, woodbury_keys, woodbury_values, key_result, keep_last = parts
    identity_block = jnp.eye(DK, dtype=jnp.float32)
    transitions = keep_last[..., None, None] * identity_block - jnp.einsum(
        "nhik,nhil->nhkl", key_result, woodbury_keys, precision=highest_precision
    )
    offsets = jnp.einsum(
        "nhik,nhiv->nhkv", key_result, woodbury_values, precision=highest_precision
    )

    def fold(accumulated, item):
        return (compose(accumulated, item), None)

    start = (jnp.broadcast_to(identity_block, (VH, DK, DK)), jnp.zeros((VH, DK, DK), jnp.float32))
    result, unused = lax.scan(fold, start, (transitions, offsets))
    return result


def finish(parts, state_in):

    def advance_block(memory_state, block):
        query_entering, scores, woodbury_keys, woodbury_values, key_result, keep_last = block
        delta_update = woodbury_values - jnp.einsum(
            "uab,ubf->uaf", woodbury_keys, memory_state, precision=highest_precision
        )
        emitted_output = jnp.einsum(
            "uab,ubf->uaf", query_entering, memory_state, precision=highest_precision
        )
        emitted_output = emitted_output + jnp.einsum(
            "hij,hjv->hiv", scores, delta_update, precision=highest_precision
        )
        memory_state = keep_last[:, None, None] * memory_state + jnp.einsum(
            "qno,qnb->qob", key_result, delta_update, precision=highest_precision
        )
        return (memory_state, emitted_output)

    state_out, emitted_output = lax.scan(advance_block, state_in, parts)
    blocks = emitted_output.shape[0]
    flat = emitted_output.transpose(0, 2, 1, 3).reshape(blocks * CH, -1)
    return (flat, state_out)


def token_layout(mixed, weight, log_decay, beta, doc_ids, out_grad):
    rows_local = mixed[0]
    docs_local = doc_ids[0]
    rim_rows, rim_docs = passed_along((rows_local[-3:], docs_local[-3:]), "seq", 1)
    rows_ext = jnp.concatenate([rim_rows, rows_local], 0).astype(jnp.float32)
    docs_ext = jnp.concatenate([rim_docs, docs_local], 0)

    def local_terms(rows_in, weight_in, decay_in, rate_in):
        return prepare(rows_in, weight_in, decay_in, rate_in, docs_ext, KH, VH // KH, DK)

    parts, prepare_pull = jax.vjp(local_terms, rows_ext, weight, log_decay[0], beta[0])
    transitions, offsets = chain_terms(parts)
    identity = (
        jnp.broadcast_to(jnp.eye(DK, dtype=jnp.float32), (VH, DK, DK)),
        jnp.zeros((VH, DK, DK), jnp.float32),
    )
    state_in = identity[1]
    for relay_step in range(SPAN):
        state_in = passed_along(advance(transitions, offsets, state_in), "seq", 1)
    (output, state_out), finish_pull = jax.vjp(finish, parts, state_in)
    cotangent = out_grad[0].astype(jnp.float32)
    parts_former, local_back = finish_pull((cotangent, jnp.zeros_like(state_out)))
    back_maps = jnp.swapaxes(transitions, 1, 2)
    state_back = identity[1]
    for relay_step in range(SPAN):
        state_back = passed_along(advance(back_maps, local_back, state_back), "seq", -1)
    parts_latter, ignored = finish_pull((jnp.zeros_like(output), state_back))
    parts_total = jax.tree.map(lambda former, latter: former + latter, parts_former, parts_latter)
    grad_rows, grad_weight, grad_decay, grad_rate = prepare_pull(parts_total)
    incoming = passed_along(grad_rows[:3].astype(jnp.bfloat16), "seq", -1).astype(jnp.float32)
    grad_local = grad_rows[3:].at[-3:].add(incoming)
    return (
        output.astype(jnp.bfloat16),
        grad_local.astype(jnp.bfloat16),
        grad_weight,
        grad_decay,
        grad_rate,
    )


def local(mixed, conv_weight, log_decay, beta, doc_ids, out_grad):
    weight = conv_weight.astype(jnp.float32)
    output, grad_local, grad_weight, grad_decay, grad_rate = token_layout(
        mixed, weight, log_decay, beta, doc_ids, out_grad
    )
    total_weight = lax.psum(grad_weight, ("dp", "seq"))
    return (output[None], grad_local[None], total_weight, grad_decay[None], grad_rate[None])


def solution(mesh):
    in_specs = (
        P("dp", "seq", None),
        P(),
        P("dp", None, "seq"),
        P("dp", None, "seq"),
        P("dp", "seq"),
        P("dp", "seq", None),
    )
    out_specs = (
        P("dp", "seq", None),
        P("dp", "seq", None),
        P(),
        P("dp", None, "seq"),
        P("dp", None, "seq"),
    )
    return jax.shard_map(local, mesh=mesh, in_specs=in_specs, out_specs=out_specs, check_vma=False)
```

profile of v0, /device:TPU:1, one launch (start us, length us, event | category | flops | bytes accessed | tf_op | source)
XLA Modules:
  0.0 849.6 jit_solution(7426034116252750742)
XLA Ops:
  8.1 4.6 collective-permute-start.1
  22.3 5.8 fusion.115
  44.5 158.4 %custom-call.10 = f32[2,16,1,64,64]{3,4,2,1,0:T(8,128)S(1)} custom-call(f32[2,16,1,64,64]{4,3,2,1,0:T(8,128)} %get-tuple-element.1184), custom_call_target="InvertDiagBlocksLowerTriangular" | custom-call | tf_op jit(solution)/shard_map/jvp(jit(_solve_triangular))/vmap(vmap())/triangular_solve | solution.py:92
  206.7 4.8 fusion.196
  211.5 5.2 multiply_subtract_fusion
  216.8 11.3 %while.87 = (s32[]{:T(128)}, f32[16,128,128]{2,1,0:T(8,128)S(1)}, f32[16,128,128]{2,1,0:T(8,128)S(1)}, f32[2,16,128,128]{3,2,1,0:T(8,128)}, f32[2,16,128,128]{3,2,1,0:T(8,128)}, /*index=5*/s32[]{:T(128)}, s32[]{:T(128)}) while((s32[]{:T(128)}, f32[16,128,128]{2,1,0:T(8,128)S(1)}, f32[16,128,128]{2,1,0:T(8,128)S(1)}, ...), condition=%wide.region_3.4_spmd.clone, body=%wide.region_2.3_spmd.clone.sunk | while | flops 805830656 | bytes 19924604 | solution.py:124
  232.7 11.7 %collective-permute-done.2 = f32[16,128,128]{2,1,0:T(8,128)S(1)} collective-permute-done((f32[16,128,128]{2,1,0:T(8,128)S(1)}, f32[16,128,128]{2,1,0:T(8,128)S(1)}, u32[]{:S(2)}, u32[]{:S(2)}) %collective-permute-start.2) | collective-permute-done | bytes 1048608 | tf_op jit(solution)/shard_map/ppermute | solution.py:20
  245.6 4.4 collective-permute-start.3
  250.0 11.7 %collective-permute-done.3 = f32[16,128,128]{2,1,0:T(8,128)S(1)} collective-permute-done((f32[16,128,128]{2,1,0:T(8,128)S(1)}, f32[16,128,128]{2,1,0:T(8,128)S(1)}, u32[]{:S(2)}, u32[]{:S(2)}) %collective-permute-start.3) | collective-permute-done | bytes 1048608 | tf_op jit(solution)/shard_map/ppermute | solution.py:20
  267.3 11.7 %collective-permute-done.4 = f32[16,128,128]{2,1,0:T(8,128)S(1)} collective-permute-done((f32[16,128,128]{2,1,0:T(8,128)S(1)}, f32[16,128,128]{2,1,0:T(8,128)S(1)}, u32[]{:S(2)}, u32[]{:S(2)}) %collective-permute-start.4) | collective-permute-done | bytes 1048608 | tf_op jit(solution)/shard_map/ppermute | solution.py:20
  280.2 4.4 collective-permute-start.5
  284.6 11.7 %collective-permute-done.5 = f32[16,128,128]{2,1,0:T(8,128)S(1)} collective-permute-done((f32[16,128,128]{2,1,0:T(8,128)S(1)}, f32[16,128,128]{2,1,0:T(8,128)S(1)}, u32[]{:S(2)}, u32[]{:S(2)}) %collective-permute-start.5) | collective-permute-done | bytes 1048608 | tf_op jit(solution)/shard_map/ppermute | solution.py:20
  297.5 4.4 collective-permute-start.6
  301.9 11.7 %collective-permute-done.6 = f32[16,128,128]{2,1,0:T(8,128)S(1)} collective-permute-done((f32[16,128,128]{2,1,0:T(8,128)S(1)}, f32[16,128,128]{2,1,0:T(8,128)S(1)}, u32[]{:S(2)}, u32[]{:S(2)}) %collective-permute-start.6) | collective-permute-done | bytes 1048608 | tf_op jit(solution)/shard_map/ppermute | solution.py:20
  314.8 4.4 collective-permute-start.7
  319.2 11.7 %collective-permute-done.7 = f32[16,128,128]{2,1,0:T(8,128)S(1)} collective-permute-done((f32[16,128,128]{2,1,0:T(8,128)S(1)}, f32[16,128,128]{2,1,0:T(8,128)S(1)}, u32[]{:S(2)}, u32[]{:S(2)}) %collective-permute-start.7) | collective-permute-done | bytes 1048608 | tf_op jit(solution)/shard_map/ppermute | solution.py:20
  332.2 4.7 collective-permute-start.8
  336.9 11.5 %collective-permute-done.8 = f32[16,128,128]{2,1,0:T(8,128)S(1)} collective-permute-done((f32[16,128,128]{2,1,0:T(8,128)S(1)}, f32[16,128,128]{2,1,0:T(8,128)S(1)}, u32[]{:S(2)}, u32[]{:S(2)}) %collective-permute-start.8) | collective-permute-done | bytes 1048608 | tf_op jit(solution)/shard_map/ppermute | solution.py:20
  368.1 16.1 %while.85 = (s32[]{:T(128)}, f32[16,128,128]{2,1,0:T(8,128)S(1)}, bf16[2,16,64,128]{3,2,1,0:T(8,128)(2,1)}, f32[2,16,128,128]{3,2,1,0:T(8,128)}, f32[2,16,64,128...) while((s32[]{:T(128)}, f32[16,128,128]{2,1,0:T(8,128)S(1)}, ...), condition=%wide.region_6.7_spmd, body=%wide.region_5.6_spmd.sunk | while | flops 705429504 | bytes 39849976 | solution.py:146
  389.8 35.1 %while.88 = (s32[]{:T(128)}, f32[16,128,128]{2,1,0:T(8,128)S(1)}, f32[2,16,64,128]{3,2,1,0:T(8,128)}, f32[2,16,64,64]{3,2,1,0:T(8,128)}, f32[2,16,64,128]{3,2,1,...) while((s32[]{:T(128)}, f32[16,128,128]{2,1,0:T(8,128)S(1)}, ...), condition=%wide.region_9.10_spmd.clone, body=%wide.region_7.9_spmd.clone.sunk | while | flops 1412038656 | bytes 87039464 | solution.py:146
  428.6 14.8 %collective-permute-done.10 = f32[16,128,128]{2,1,0:T(8,128)S(1)} collective-permute-done((f32[16,128,128]{2,1,0:T(8,128)S(1)}, f32[16,128,128]{2,1,0:T(8,128)S(1)}, u32[]{:S(2)}, u32[]{:S(2)}) %collective-permute-start.10) | collective-permute-done | bytes 1048608 | tf_op jit(solution)/shard_map/ppermute | solution.py:20
  447.3 14.2 %collective-permute-done.11 = f32[16,128,128]{2,1,0:T(8,128)S(1)} collective-permute-done((f32[16,128,128]{2,1,0:T(8,128)S(1)}, f32[16,128,128]{2,1,0:T(8,128)S(1)}, u32[]{:S(2)}, u32[]{:S(2)}) %collective-permute-start.11) | collective-permute-done | bytes 1048608 | tf_op jit(solution)/shard_map/ppermute | solution.py:20
  465.3 14.2 %collective-permute-done.12 = f32[16,128,128]{2,1,0:T(8,128)S(1)} collective-permute-done((f32[16,128,128]{2,1,0:T(8,128)S(1)}, f32[16,128,128]{2,1,0:T(8,128)S(1)}, u32[]{:S(2)}, u32[]{:S(2)}) %collective-permute-start.12) | collective-permute-done | bytes 1048608 | tf_op jit(solution)/shard_map/ppermute | solution.py:20
  483.3 14.2 %collective-permute-done.13 = f32[16,128,128]{2,1,0:T(8,128)S(1)} collective-permute-done((f32[16,128,128]{2,1,0:T(8,128)S(1)}, f32[16,128,128]{2,1,0:T(8,128)S(1)}, u32[]{:S(2)}, u32[]{:S(2)}) %collective-permute-start.13) | collective-permute-done | bytes 1048608 | tf_op jit(solution)/shard_map/ppermute | solution.py:20
  501.3 14.2 %collective-permute-done.14 = f32[16,128,128]{2,1,0:T(8,128)S(1)} collective-permute-done((f32[16,128,128]{2,1,0:T(8,128)S(1)}, f32[16,128,128]{2,1,0:T(8,128)S(1)}, u32[]{:S(2)}, u32[]{:S(2)}) %collective-permute-start.14) | collective-permute-done | bytes 1048608 | tf_op jit(solution)/shard_map/ppermute | solution.py:20
  519.3 14.2 %collective-permute-done.15 = f32[16,128,128]{2,1,0:T(8,128)S(1)} collective-permute-done((f32[16,128,128]{2,1,0:T(8,128)S(1)}, f32[16,128,128]{2,1,0:T(8,128)S(1)}, u32[]{:S(2)}, u32[]{:S(2)}) %collective-permute-start.15) | collective-permute-done | bytes 1048608 | tf_op jit(solution)/shard_map/ppermute | solution.py:20
  537.5 14.2 %collective-permute-done.16 = f32[16,128,128]{2,1,0:T(8,128)S(1)} collective-permute-done((f32[16,128,128]{2,1,0:T(8,128)S(1)}, f32[16,128,128]{2,1,0:T(8,128)S(1)}, u32[]{:S(2)}, u32[]{:S(2)}) %collective-permute-start.16) | collective-permute-done | bytes 1048608 | tf_op jit(solution)/shard_map/ppermute | solution.py:20
  558.3 12.6 %collective-permute-done.17 = f32[16,128,128]{2,1,0:T(8,128)S(1)} collective-permute-done((f32[16,128,128]{2,1,0:T(8,128)}, f32[16,128,128]{2,1,0:T(8,128)S(1)}, u32[]{:S(2)}, u32[]{:S(2)}) %collective-permute-start.17) | collective-permute-done | bytes 1048608 | tf_op jit(solution)/shard_map/ppermute | solution.py:20
  576.5 31.9 %while.86 = (s32[]{:T(128)}, f32[16,128,128]{2,1,0:T(8,128)S(1)}, f32[2,16,64,128]{3,2,1,0:T(8,128)}, f32[2,16,64,64]{3,2,1,0:T(8,128)}, f32[2,16,64,128]{3,2,1,...) while((s32[]{:T(128)}, f32[16,128,128]{2,1,0:T(8,128)S(1)}, ...), condition=%wide.region_12.13_spmd, body=%wide.region_10.12_spmd.sunk | while | flops 1410990080 | bytes 67115376 | solution.py:146
  646.5 9.9 %multiply_reduce_fusion.3 = (f32[4096]{0:T(1024)S(1)}, f32[4096]{0:T(1024)S(1)}, f32[4096]{0:T(1024)S(1)}, f32[4096]{0:T(1024)S(1)}, f32[128,4096]{0,1:T(8,128)S(1)}) fusion(f32[131,4096]{0,1:T(8,128)} %copy-done.10, pred[128]{0:T(512)(128)(4,1)S(1)} %copy-done.99, pred[128]{0:T(512)(128)(4,1)S(1)} %copy-done.95, pred[128]{0:T(512)(128)(4,1)S(1)} %copy-done.97, ...), kind=kLoop, calls=%fused_computation.156 | loop fusion | flops 11517952 | bytes 14745984 | tf_op jit(solution)/shard_map/transpose(jvp())/reduce_sum | solution.py:52
  673.2 11.0 %scatter-add.4 = bf16[128,4096]{0,1:T(8,128)(2,1)} dynamic-update-slice(bf16[128,4096]{0,1:T(8,128)(2,1)} %slice.163, bf16[3,4096]{0,1:T(8,128)(2,1)S(1)} %slice_add_fusion, s32[]{:T(128)} %constant.228.clone.1, s32[]{:T(128)} %constant.221.clone.1) | dynamic-update-slice | bytes 49156 | tf_op jit(solution)/shard_map/scatter-add | solution.py:182
  686.4 154.6 %all-reduce.17.cloned.1.call-done = f32[4,4096]{1,0:T(4,128)} async-done(((f32[4,4096]{1,0:T(4,128)}), f32[4,4096]{1,0:T(4,128)}) %all-reduce.17.cloned.1.call-update) | async-done | bytes 65552 | tf_op jit(solution)/shard_map/psum | solution.py:197
  (515 shorter events, 260.8 us)
Async XLA Ops:
  7.2 10.7 %copy-start.106 = (s32[1,128]{1,0:T(1,128)S(1)}, s32[1,128]{1,0:T(1,128)}, u32[]{:S(2)}) copy-start(s32[1,128]{1,0:T(1,128)} %param.20) | copy-start | bytes 1540
  7.2 9.9 %copy-start.87 = (bf16[4,4096]{1,0:T(4,128)(2,1)S(1)}, bf16[4,4096]{1,0:T(4,128)(2,1)}, u32[]{:S(2)}) copy-start(bf16[4,4096]{1,0:T(4,128)(2,1)} %param.17) | copy-start | bytes 98308
  7.2 10.0 %copy-start.102 = (f32[1,16,128]{2,1,0:T(8,128)S(1)}, f32[1,16,128]{2,1,0:T(8,128)}, u32[]{:S(2)}) copy-start(f32[1,16,128]{2,1,0:T(8,128)} %param.19) | copy-start | bytes 24580
  7.2 10.1 %copy-start.103 = (f32[1,16,128]{2,1,0:T(8,128)S(1)}, f32[1,16,128]{2,1,0:T(8,128)}, u32[]{:S(2)}) copy-start(f32[1,16,128]{2,1,0:T(8,128)} %param.18) | copy-start | bytes 24580
  7.2 833.8 %all-reduce.17.cloned.1.call-start = ((), (), s32[]{:S(2)}) async-start(), calls=%async_computation | async-start | bytes 131072 | tf_op jit(solution)/shard_map/psum | solution.py:197
  8.1 12.8 %collective-permute-start.1 = (bf16[3,4096]{1,0:T(4,128)(2,1)S(1)}, bf16[3,4096]{1,0:T(4,128)(2,1)S(1)}, u32[]{:S(2)}, u32[]{:S(2)}) collective-permute-start(bf16[3,4096]{1,0:T(4,128)(2,1)S(1)} %slice_bitcast_fusion), channel_id=1, source_target_pairs={{0,1},{1,2},{2,3},{3,4},{4,5},{5,6},{6,7},{7,8},{8,9},{9,10},{10,1... | collective-permute-start | bytes 73736 | tf_op jit(solution)/shard_map/ppermute | solution.py:20
  13.4 6.2 collective-permute-start
  37.6 165.4 %copy-start.18 = (f32[128,8,2,128]{3,0,2,1:T(8,128)}, f32[128,8,2,128]{3,0,2,1:T(8,128)S(1)}, u32[]{:S(2)}) copy-start(f32[128,8,2,128]{3,0,2,1:T(8,128)S(1)} %broadcast_in_dim.266) | copy-start | bytes 3145732
  203.6 7.9 copy-start.6
  229.1 15.3 %collective-permute-start.2 = (f32[16,128,128]{2,1,0:T(8,128)S(1)}, f32[16,128,128]{2,1,0:T(8,128)S(1)}, u32[]{:S(2)}, u32[]{:S(2)}) collective-permute-start(f32[16,128,128]{2,1,0:T(8,128)S(1)} %convolution_add_fusion.26), channel_id=1, source_target_pairs={{0,1},{1,2},{2,3},{3,4},{4,5},{5,6},{6,7},{7,8},{8,9},{9,10},{10,1... | collective-permute-start | bytes 3145736 | tf_op jit(solution)/shard_map/ppermute | solution.py:20
  245.6 16.1 %collective-permute-start.3 = (f32[16,128,128]{2,1,0:T(8,128)S(1)}, f32[16,128,128]{2,1,0:T(8,128)S(1)}, u32[]{:S(2)}, u32[]{:S(2)}) collective-permute-start(f32[16,128,128]{2,1,0:T(8,128)S(1)} %convolution_add_fusion.25), channel_id=1, source_target_pairs={{0,1},{1,2},{2,3},{3,4},{4,5},{5,6},{6,7},{7,8},{8,9},{9,10},{10,1... | collective-permute-start | bytes 3145736 | tf_op jit(solution)/shard_map/ppermute | solution.py:20
  262.9 16.1 %collective-permute-start.4 = (f32[16,128,128]{2,1,0:T(8,128)S(1)}, f32[16,128,128]{2,1,0:T(8,128)S(1)}, u32[]{:S(2)}, u32[]{:S(2)}) collective-permute-start(f32[16,128,128]{2,1,0:T(8,128)S(1)} %convolution_add_fusion.24), channel_id=1, source_target_pairs={{0,1},{1,2},{2,3},{3,4},{4,5},{5,6},{6,7},{7,8},{8,9},{9,10},{10,1... | collective-permute-start | bytes 3145736 | tf_op jit(solution)/shard_map/ppermute | solution.py:20
  280.2 16.1 %collective-permute-start.5 = (f32[16,128,128]{2,1,0:T(8,128)S(1)}, f32[16,128,128]{2,1,0:T(8,128)S(1)}, u32[]{:S(2)}, u32[]{:S(2)}) collective-permute-start(f32[16,128,128]{2,1,0:T(8,128)S(1)} %convolution_add_fusion.23), channel_id=1, source_target_pairs={{0,1},{1,2},{2,3},{3,4},{4,5},{5,6},{6,7},{7,8},{8,9},{9,10},{10,1... | collective-permute-start | bytes 3145736 | tf_op jit(solution)/shard_map/ppermute | solution.py:20
  297.5 16.1 %collective-permute-start.6 = (f32[16,128,128]{2,1,0:T(8,128)S(1)}, f32[16,128,128]{2,1,0:T(8,128)S(1)}, u32[]{:S(2)}, u32[]{:S(2)}) collective-permute-start(f32[16,128,128]{2,1,0:T(8,128)S(1)} %convolution_add_fusion.22), channel_id=1, source_target_pairs={{0,1},{1,2},{2,3},{3,4},{4,5},{5,6},{6,7},{7,8},{8,9},{9,10},{10,1... | collective-permute-start | bytes 3145736 | tf_op jit(solution)/shard_map/ppermute | solution.py:20
  314.8 16.1 %collective-permute-start.7 = (f32[16,128,128]{2,1,0:T(8,128)S(1)}, f32[16,128,128]{2,1,0:T(8,128)S(1)}, u32[]{:S(2)}, u32[]{:S(2)}) collective-permute-start(f32[16,128,128]{2,1,0:T(8,128)S(1)} %convolution_add_fusion.21), channel_id=1, source_target_pairs={{0,1},{1,2},{2,3},{3,4},{4,5},{5,6},{6,7},{7,8},{8,9},{9,10},{10,1... | collective-permute-start | bytes 3145736 | tf_op jit(solution)/shard_map/ppermute | solution.py:20
  332.2 22.8 %copy-start.76 = (bf16[1,128,2048]{2,1,0:T(8,128)(2,1)S(1)}, bf16[1,128,2048]{2,1,0:T(8,128)(2,1)}, u32[]{:S(2)}) copy-start(bf16[1,128,2048]{2,1,0:T(8,128)(2,1)} %param.21) | copy-start | bytes 1572868
  332.2 16.2 %collective-permute-start.8 = (f32[16,128,128]{2,1,0:T(8,128)S(1)}, f32[16,128,128]{2,1,0:T(8,128)S(1)}, u32[]{:S(2)}, u32[]{:S(2)}) collective-permute-start(f32[16,128,128]{2,1,0:T(8,128)S(1)} %convolution_add_fusion.20), channel_id=1, source_target_pairs={{0,1},{1,2},{2,3},{3,4},{4,5},{5,6},{6,7},{7,8},{8,9},{9,10},{10,1... | collective-permute-start | bytes 3145736 | tf_op jit(solution)/shard_map/ppermute | solution.py:20
  350.6 16.4 %collective-permute-start.9 = (f32[16,128,128]{2,1,0:T(8,128)}, f32[16,128,128]{2,1,0:T(8,128)S(1)}, u32[]{:S(2)}, u32[]{:S(2)}) collective-permute-start(f32[16,128,128]{2,1,0:T(8,128)} %convolution_add_fusion.19), channel_id=1, source_target_pairs={{0,1},{1,2},{2,3},{3,4},{4,5},{5,6},{6,7},{7,8},{8,9},{9,10},{10,1... | collective-permute-start | bytes 3145736 | tf_op jit(solution)/shard_map/ppermute | solution.py:20
  426.7 16.8 %collective-permute-start.10 = (f32[16,128,128]{2,1,0:T(8,128)S(1)}, f32[16,128,128]{2,1,0:T(8,128)S(1)}, u32[]{:S(2)}, u32[]{:S(2)}) collective-permute-start(f32[16,128,128]{2,1,0:T(8,128)S(1)} %convolution_add_fusion.18), channel_id=1, source_target_pairs={{1,0},{2,1},{3,2},{4,3},{5,4},{6,5},{7,6},{8,7},{9,8},{10,9},{11,1... | collective-permute-start | bytes 3145736 | tf_op jit(solution)/shard_map/ppermute | solution.py:20
  445.4 16.1 %collective-permute-start.11 = (f32[16,128,128]{2,1,0:T(8,128)S(1)}, f32[16,128,128]{2,1,0:T(8,128)S(1)}, u32[]{:S(2)}, u32[]{:S(2)}) collective-permute-start(f32[16,128,128]{2,1,0:T(8,128)S(1)} %convolution_add_fusion.17), channel_id=1, source_target_pairs={{1,0},{2,1},{3,2},{4,3},{5,4},{6,5},{7,6},{8,7},{9,8},{10,9},{11,1... | collective-permute-start | bytes 3145736 | tf_op jit(solution)/shard_map/ppermute | solution.py:20
  463.4 16.1 %collective-permute-start.12 = (f32[16,128,128]{2,1,0:T(8,128)S(1)}, f32[16,128,128]{2,1,0:T(8,128)S(1)}, u32[]{:S(2)}, u32[]{:S(2)}) collective-permute-start(f32[16,128,128]{2,1,0:T(8,128)S(1)} %convolution_add_fusion.16), channel_id=1, source_target_pairs={{1,0},{2,1},{3,2},{4,3},{5,4},{6,5},{7,6},{8,7},{9,8},{10,9},{11,1... | collective-permute-start | bytes 3145736 | tf_op jit(solution)/shard_map/ppermute | solution.py:20
  481.4 16.1 %collective-permute-start.13 = (f32[16,128,128]{2,1,0:T(8,128)S(1)}, f32[16,128,128]{2,1,0:T(8,128)S(1)}, u32[]{:S(2)}, u32[]{:S(2)}) collective-permute-start(f32[16,128,128]{2,1,0:T(8,128)S(1)} %convolution_add_fusion.15), channel_id=1, source_target_pairs={{1,0},{2,1},{3,2},{4,3},{5,4},{6,5},{7,6},{8,7},{9,8},{10,9},{11,1... | collective-permute-start | bytes 3145736 | tf_op jit(solution)/shard_map/ppermute | solution.py:20
  499.4 16.1 %collective-permute-start.14 = (f32[16,128,128]{2,1,0:T(8,128)S(1)}, f32[16,128,128]{2,1,0:T(8,128)S(1)}, u32[]{:S(2)}, u32[]{:S(2)}) collective-permute-start(f32[16,128,128]{2,1,0:T(8,128)S(1)} %convolution_add_fusion.14), channel_id=1, source_target_pairs={{1,0},{2,1},{3,2},{4,3},{5,4},{6,5},{7,6},{8,7},{9,8},{10,9},{11,1... | collective-permute-start | bytes 3145736 | tf_op jit(solution)/shard_map/ppermute | solution.py:20
  517.4 16.1 %collective-permute-start.15 = (f32[16,128,128]{2,1,0:T(8,128)S(1)}, f32[16,128,128]{2,1,0:T(8,128)S(1)}, u32[]{:S(2)}, u32[]{:S(2)}) collective-permute-start(f32[16,128,128]{2,1,0:T(8,128)S(1)} %convolution_add_fusion.13), channel_id=1, source_target_pairs={{1,0},{2,1},{3,2},{4,3},{5,4},{6,5},{7,6},{8,7},{9,8},{10,9},{11,1... | collective-permute-start | bytes 3145736 | tf_op jit(solution)/shard_map/ppermute | solution.py:20
  535.4 21.5 %copy-start.75 = (bf16[2,16,64,128]{3,2,1,0:T(8,128)(2,1)S(1)}, bf16[2,16,64,128]{3,2,1,0:T(8,128)(2,1)}, u32[]{:S(2)}) copy-start(bf16[2,16,64,128]{3,2,1,0:T(8,128)(2,1)} %get-tuple-element.728) | copy-start | bytes 1572868
  535.4 16.2 %collective-permute-start.16 = (f32[16,128,128]{2,1,0:T(8,128)S(1)}, f32[16,128,128]{2,1,0:T(8,128)S(1)}, u32[]{:S(2)}, u32[]{:S(2)}) collective-permute-start(f32[16,128,128]{2,1,0:T(8,128)S(1)} %convolution_add_fusion.12), channel_id=1, source_target_pairs={{1,0},{2,1},{3,2},{4,3},{5,4},{6,5},{7,6},{8,7},{9,8},{10,9},{11,1... | collective-permute-start | bytes 3145736 | tf_op jit(solution)/shard_map/ppermute | solution.py:20
  554.6 16.3 %collective-permute-start.17 = (f32[16,128,128]{2,1,0:T(8,128)}, f32[16,128,128]{2,1,0:T(8,128)S(1)}, u32[]{:S(2)}, u32[]{:S(2)}) collective-permute-start(f32[16,128,128]{2,1,0:T(8,128)} %convolution_add_fusion.11), channel_id=1, source_target_pairs={{1,0},{2,1},{3,2},{4,3},{5,4},{6,5},{7,6},{8,7},{9,8},{10,9},{11,1... | collective-permute-start | bytes 3145736 | tf_op jit(solution)/shard_map/ppermute | solution.py:20
  646.4 9.9 %copy-start.80 = (f32[1,4096]{1,0:T(1,128)S(1)}, f32[1,4096]{1,0:T(1,128)}, u32[]{:S(2)}) copy-start(f32[1,4096]{1,0:T(1,128)} %copy-done.79) | copy-start | bytes 49156
  646.5 9.9 %copy-start.82 = (f32[1,4096]{1,0:T(1,128)S(1)}, f32[1,4096]{1,0:T(1,128)}, u32[]{:S(2)}) copy-start(f32[1,4096]{1,0:T(1,128)} %copy-done.81) | copy-start | bytes 49156
  646.5 9.9 %copy-start.84 = (f32[1,4096]{1,0:T(1,128)S(1)}, f32[1,4096]{1,0:T(1,128)}, u32[]{:S(2)}) copy-start(f32[1,4096]{1,0:T(1,128)} %copy-done.83) | copy-start | bytes 49156
  646.5 9.9 %copy-start.86 = (f32[1,4096]{1,0:T(1,128)S(1)}, f32[1,4096]{1,0:T(1,128)}, u32[]{:S(2)}) copy-start(f32[1,4096]{1,0:T(1,128)} %copy-done.85) | copy-start | bytes 49156
  665.1 5.8 collective-permute-start.18
  (133 other events, 365.3 us)
Sparse Core Ops, SparseCore 0:
  667.9 173.1 all-reduce.16
where the time goes:
time: 858 us; the launch traced here: 850 us
  waiting for transfers between devices  350 us (41%)
  other arithmetic  208 us (24%)
  matrix products  131 us (15%)
  local copies, waits for them, and re-layouts  84 us (10%)
  starting transfers between devices  59 us (7%)
  between operations  15.6 us (2%)
    ppermute x19, waiting for transfers between devices, passed_along(): return lax.ppermute(array, axis, pairs)  195 us
    another operation x4, other arithmetic, prepare(): jax.scipy.linalg.solve_triangular(triangle, right_side, lower=True, unit_...  159 us
    psum x1, waiting for transfers between devices, local(): total_weight = lax.psum(grad_weight, ('dp', 'seq'))  155 us
    ppermute x19, starting transfers between devices, passed_along(): return lax.ppermute(array, axis, pairs)  58.9 us
    dot_general x16, matrix products, advance(): jnp.einsum('hij,hjk->hik', transition, carried, precision=highest_precision)  26.3 us
    dot_general x10, matrix products, advance_block(): jnp.einsum('uab,ubf->uaf', woodbury_keys, memory_state, precision=highest...  20.2 us
    dot_general x10, matrix products, advance_block(): jnp.einsum('qno,qnb->qob', key_result, delta_update, precision=highest_pr...  18.3 us
    dot_general x10, matrix products, advance_block(): jnp.einsum('uab,ubf->uaf', query_entering, memory_state, precision=highes...  18.3 us
  transfers between devices with their start and end apart: 20, of which 17 were waited for; matrix products, arithmetic and copies ran while one was open for 4% of the time, Pallas kernels for 0%

commit v1 on v0

v1 whole, which is shorter than its diff:
```python
import functools

import jax
import jax.numpy as jnp
from jax import lax
from jax.experimental import pallas as pl
from jax.experimental.pallas import tpu as pltpu
from jax.sharding import PartitionSpec as P

DK = 128
KH = 8
VH = 16
L = 128
GROUP = 8
QUARTER = GROUP * 128
NB = QUARTER // L
PER = 2
EPS = 1e-6

f32 = jnp.float32
bf16 = jnp.bfloat16
NN = (((1,), (0,)), ((), ()))
NT = (((1,), (1,)), ((), ()))
MESH = pl.DeviceIdType.MESH
VM = pltpu.VMEM
vspec = pl.BlockSpec(memory_space=pltpu.VMEM)
sspec = pl.BlockSpec(memory_space=pltpu.SMEM)


def split(a):
    high = a.astype(bf16)
    return high, (a - high.astype(f32)).astype(bf16)


def one(a):
    return (a.astype(bf16),)


def mm(a, b, dims=NN):
    def dot(p, q):
        return lax.dot_general(p, q, dims, preferred_element_type=f32)

    total = dot(a[0], b[0])
    if len(b) > 1:
        total = total + dot(a[0], b[1])
    if len(a) > 1:
        total = total + dot(a[1], b[0])
    return total


def exact(a, b):
    return lax.dot_general(a, b, NN, preferred_element_type=f32, precision=lax.Precision.HIGHEST)


def iotas():
    return (
        lax.broadcasted_iota(jnp.int32, (L, L), 0),
        lax.broadcasted_iota(jnp.int32, (L, L), 1),
    )


def heads_kernel(
    mixed, grad, aux, out_mixed, out_grad, out_aux, halo_mixed, halo_aux, send, recv, hsend, hrecv
):
    dp = lax.axis_index("dp")
    me = lax.axis_index("seq")
    row, j = me // GROUP, lax.rem(me, GROUP)
    base = row * GROUP
    last = GROUP - 1
    before = lax.rem(row + 3, 4) * GROUP
    after = lax.rem(row + 1, 4) * GROUP
    is_last = j == last

    barrier = pltpu.get_barrier_semaphore()
    for s in range(1, GROUP):
        pl.semaphore_signal(
            barrier, inc=1, device_id=(dp, base + lax.rem(j + s, GROUP)), device_id_type=MESH
        )
    pl.semaphore_signal(barrier, inc=1, device_id=(dp, before + last), device_id_type=MESH)
    pl.semaphore_wait(barrier, jnp.where(is_last, 2 * GROUP - 1, GROUP - 1))

    def pieces(to, start, rows):
        q = pl.ds(pl.multiple_of(to * DK, DK), DK)
        k = pl.ds(pl.multiple_of((KH + to) * DK, DK), DK)
        v = pl.ds(pl.multiple_of((2 * KH + 2 * to) * DK, 2 * DK), 2 * DK)
        r = pl.ds(start, rows)
        return mixed.at[r, q], mixed.at[r, k], mixed.at[r, v]

    copies = []
    place = pl.ds(pl.multiple_of(j * 128, 128), 128)
    for s in range(1, GROUP):
        to = lax.rem(j + s, GROUP)
        q, k, v = pieces(to, 0, 128)
        g = grad.at[:, pl.ds(pl.multiple_of(to * 2 * DK, 2 * DK), 2 * DK)]
        pairs = (
            (q, out_mixed.at[place, pl.ds(0, DK)]),
            (k, out_mixed.at[place, pl.ds(DK, DK)]),
            (v, out_mixed.at[place, pl.ds(2 * DK, 2 * DK)]),
            (aux.at[to], out_aux.at[j]),
            (g, out_grad.at[place, :]),
        )
        for i, (src, dst) in enumerate(pairs):
            copy = pltpu.make_async_remote_copy(
                src_ref=src,
                dst_ref=dst,
                send_sem=send.at[s, i],
                recv_sem=recv.at[s, i],
                device_id=(dp, base + to),
                device_id_type=MESH,
            )
            copy.start()
            copies.append(copy)

    def halo_copies(to):
        q, k, v = pieces(to, 112, 16)
        pairs = (
            (q, halo_mixed.at[:, pl.ds(0, DK)]),
            (k, halo_mixed.at[:, pl.ds(DK, DK)]),
            (v, halo_mixed.at[:, pl.ds(2 * DK, 2 * DK)]),
            (aux.at[to], halo_aux.at[:, :]),
        )
        return [
            pltpu.make_async_remote_copy(
                src_ref=src,
                dst_ref=dst,
                send_sem=hsend.at[to, i],
                recv_sem=hrecv.at[i],
                device_id=(dp, after + to),
                device_id_type=MESH,
            )
            for i, (src, dst) in enumerate(pairs)
        ]

    @pl.when(is_last)
    def _():
        for to in range(GROUP):
            for copy in halo_copies(to):
                copy.start()

    out_mixed[place, 0:DK] = mixed[:, pl.ds(pl.multiple_of(j * DK, DK), DK)]
    out_mixed[place, DK : 2 * DK] = mixed[:, pl.ds(pl.multiple_of((KH + j) * DK, DK), DK)]
    out_mixed[place, 2 * DK :] = mixed[
        :, pl.ds(pl.multiple_of((2 * KH + 2 * j) * DK, 2 * DK), 2 * DK)
    ]
    out_grad[place, :] = grad[:, pl.ds(pl.multiple_of(j * 2 * DK, 2 * DK), 2 * DK)]
    out_aux[j] = aux[j]

    for copy in copies:
        copy.wait()
    for copy in halo_copies(0):
        copy.wait_recv()

    @pl.when(is_last)
    def _():
        for to in range(GROUP):
            for copy in halo_copies(to):
                copy.wait_send()


def to_heads(mixed, grad, aux):
    return pl.pallas_call(
        heads_kernel,
        out_shape=(
            jax.ShapeDtypeStruct((QUARTER, 4 * DK), bf16),
            jax.ShapeDtypeStruct((QUARTER, 2 * DK), bf16),
            jax.ShapeDtypeStruct((GROUP, 8, 128), f32),
            jax.ShapeDtypeStruct((16, 4 * DK), bf16),
            jax.ShapeDtypeStruct((8, 128), f32),
        ),
        in_specs=[vspec] * 3,
        out_specs=(vspec,) * 5,
        scratch_shapes=[
            pltpu.SemaphoreType.DMA((GROUP, 5)),
            pltpu.SemaphoreType.DMA((GROUP, 5)),
            pltpu.SemaphoreType.DMA((GROUP, 4)),
            pltpu.SemaphoreType.DMA((4,)),
        ],
        compiler_params=pltpu.CompilerParams(collective_id=0, has_side_effects=True),
        name="to_heads",
    )(mixed, grad, aux)


def gates(tile, h, doc_column, doc_row, doc_before, columns):
    ri, ci = iotas()
    cum = columns[:, h : h + 1]
    cum_row = tile[h : h + 1, :]
    rate = columns[:, 2 + h : 3 + h]
    cum_last = tile[h : h + 1, L - 1 : L]
    doc_last = tile[4:5, L - 1 : L]
    same = doc_column == doc_row
    fade = jnp.where(same & (ri >= ci), jnp.exp(jnp.minimum(cum - cum_row, 0.0)), 0.0)
    carry = doc_column == doc_before
    enter = jnp.where(carry, jnp.exp(cum), 0.0)
    tail = jnp.where(doc_column == doc_last, jnp.exp(cum_last - cum), 0.0)
    keep = jnp.where(doc_last == doc_before, jnp.exp(cum_last), 0.0)
    return fade, enter, tail, keep, rate


def first_kernel(
    meta, mixed, halo, grad, aux, halo_aux, weight, summed_o, q_o, k_o, tile_o, col_o, t_o, w_o, u_o,
    p_o, a_o, b_o, r_o, send_o, xs, ds,
):
    j, first = meta[0], meta[1]
    ri, ci = iotas()
    upper = jnp.where(ri <= ci, 1.0, 0.0).astype(f32)
    flat = aux[...].reshape(NB * 8, 128)
    sums = exact(flat, upper)
    which = lax.rem(lax.broadcasted_iota(jnp.int32, (NB * 8, 128), 0), 8)
    tile_o[...] = jnp.where(which < 2, sums, flat).reshape(NB, 8, 128)

    rows = PER * L
    halo_columns = jnp.transpose(halo_aux[...])
    halo_columns = jnp.where(first == 1, -1.0, halo_columns)
    xs[0:8, :] = halo[8:16, :].astype(f32)
    ds[0:8, :] = halo_columns[120:128, :]
    col_o[0:8, :] = halo_columns[120:128, :]

    wq = weight[:, pl.ds(pl.multiple_of(j * DK, DK), DK)].astype(f32)
    wk = weight[:, pl.ds(pl.multiple_of((KH + j) * DK, DK), DK)].astype(f32)
    wv = weight[:, pl.ds(pl.multiple_of((2 * KH + 2 * j) * DK, 2 * DK), 2 * DK)].astype(f32)
    taps = jnp.concatenate([wq, wk, wv], axis=1)

    def body(i, carry):
        r0 = pl.multiple_of(i * rows, rows)
        xs[8:, :] = mixed[pl.ds(r0, rows), :].astype(f32)
        tiles = [tile_o[i * PER + p] for p in range(PER)]
        for p in range(PER):
            ds[8 + p * L : 8 + (p + 1) * L, :] = jnp.transpose(tiles[p])
        col_o[pl.ds(pl.multiple_of(r0 + 8, 8), rows), :] = ds[8:, :]
        doc = ds[8:, 4:5]
        summed = taps[3:4, :] * xs[8:, :]
        for o in (1, 2, 3):
            same = ds[8 - o : 8 - o + rows, 4:5] == doc
            summed = summed + taps[3 - o : 4 - o, :] * jnp.where(
                same, xs[8 - o : 8 - o + rows, :], 0.0
            )
        summed_o[pl.ds(r0, rows), :] = summed
        active = summed / (1.0 + jnp.exp(-summed))
        q = active[:, :DK]
        k = active[:, DK : 2 * DK]
        q = q * lax.rsqrt(jnp.sum(q * q, -1, keepdims=True) + EPS) * DK**-0.5
        k = k * lax.rsqrt(jnp.sum(k * k, -1, keepdims=True) + EPS)
        q_o[pl.ds(r0, rows), :] = q
        k_o[pl.ds(r0, rows), :] = k

        chains = []
        for p in range(PER):
            lo = slice(p * L, (p + 1) * L)
            kp, qp = k[lo], q[lo]
            ks, qs = split(kp), split(qp)
            inner = mm(ks, ks, NT)
            score = mm(qs, ks, NT)
            doc_column = ds[8 + p * L : 8 + (p + 1) * L, 4:5]
            doc_row = tiles[p][4:5, :]
            doc_before = ds[7 + p * L : 8 + p * L, 4:5]
            columns = ds[8 + p * L : 8 + (p + 1) * L, :]
            for h in range(2):
                fade, enter, tail, keep, rate = gates(
                    tiles[p], h, doc_column, doc_row, doc_before, columns
                )
                low = jnp.where(ri > ci, rate * inner * fade, 0.0)
                vp = active[lo, (2 + h) * DK : (3 + h) * DK]
                chains.append(
                    dict(p=p, h=h, low=low, score=score * fade, enter=enter, tail=tail, keep=keep,
                         rate=rate, k=kp, q=qp, v=vp)
                )
        eye = jnp.where(ri == ci, 1.0, 0.0).astype(f32)
        size = 1
        inverse = None
        while size < L:
            mask = (ri // (2 * size) == ci // (2 * size)) & (
                lax.rem(ri // size, 2) == 1
            ) & (lax.rem(ci // size, 2) == 0)
            corners = [jnp.where(mask, c["low"], 0.0) for c in chains]
            if inverse is None:
                inverse = [eye - x for x in corners]
            else:
                parts = [split(x) for x in inverse]
                inner = [mm(split(c), x) for c, x in zip(corners, parts)]
                inverse = [
                    x - mm(y, split(z)) for x, y, z in zip(inverse, parts, inner)
                ]
            size *= 2
        for c, t in zip(chains, inverse):
            n = (i * PER + c["p"]) * 2 + c["h"]
            t_o[n] = t
            p_o[n] = c["score"]
            ts = split(t)
            w = mm(ts, split((c["rate"] * c["enter"]) * c["k"]))
            u = mm(ts, split(c["rate"] * c["v"]))
            w_o[n] = w
            u_o[n] = u
            kt = jnp.transpose(c["tail"] * c["k"])
            kts = split(kt)
            ws = split(w)
            a_o[n] = jnp.where(ri == ci, c["keep"], 0.0) - mm(kts, ws)
            b_o[n] = mm(split(jnp.transpose(u)), split(c["tail"] * c["k"]))
            g = grad[pl.ds(pl.multiple_of(r0 + c["p"] * L, L), L), c["h"] * DK : (c["h"] + 1) * DK]
            du = mm(split(jnp.transpose(c["score"])), (g,))
            gt = (jnp.transpose(g.astype(f32)).astype(bf16),)
            r_o[n] = mm(gt, split(c["enter"] * c["q"])) - mm(split(jnp.transpose(du)), ws)
        xs[0:8, :] = xs[rows : rows + 8, :]
        ds[0:8, :] = ds[rows : rows + 8, :]
        return carry

    lax.fori_loop(0, NB // PER, body, 0)

    def scan(i, carry):
        s0, s1, r0, r1 = carry
        m = NB - 1 - i
        out = []
        for h, s in ((0, s0), (1, s1)):
            out.append(mm(split(s), split(a_o[2 * i + h]), NT) + b_o[2 * i + h])
        for h, r in ((0, r0), (1, r1)):
            out.append(mm(split(r), split(a_o[2 * m + h])) + r_o[2 * m + h])
        return tuple(out)

    zero = jnp.zeros((DK, DK), f32)
    states = lax.fori_loop(0, NB, scan, (zero,) * 4)
    for i in range(4):
        send_o[i] = states[i]


def first_phase(meta, mixed, halo, grad, aux, halo_aux, weight, interpret=False):
    square = jax.ShapeDtypeStruct((2 * NB, DK, DK), f32)
    return pl.pallas_call(
        first_kernel,
        out_shape=(
            jax.ShapeDtypeStruct((QUARTER, 4 * DK), f32),
            jax.ShapeDtypeStruct((QUARTER, DK), f32),
            jax.ShapeDtypeStruct((QUARTER, DK), f32),
            jax.ShapeDtypeStruct((NB, 8, 128), f32),
            jax.ShapeDtypeStruct((8 + QUARTER, 8), f32),
        )
        + (square,) * 7
        + (jax.ShapeDtypeStruct((4, DK, DK), f32),),
        in_specs=[sspec] + [vspec] * 6,
        out_specs=(vspec,) * 13,
        scratch_shapes=[VM((8 + PER * L, 4 * DK), f32), VM((8 + PER * L, 8), f32)],
        compiler_params=pltpu.CompilerParams(vmem_limit_bytes=60 * 1024 * 1024),
        name="first_phase",
        interpret=interpret,
    )(meta, mixed, halo, grad, aux, halo_aux, weight)


def states_kernel(src, dst, send, recv):
    dp = lax.axis_index("dp")
    me = lax.axis_index("seq")
    after = lax.rem(me + GROUP, 4 * GROUP)
    before = lax.rem(me + 3 * GROUP, 4 * GROUP)
    barrier = pltpu.get_barrier_semaphore()
    for to in (after, before):
        pl.semaphore_signal(barrier, inc=1, device_id=(dp, to), device_id_type=MESH)
    pl.semaphore_wait(barrier, 2)
    copies = []
    for i, to in ((0, after), (1, before)):
        copy = pltpu.make_async_remote_copy(
            src_ref=src.at[pl.ds(2 * i, 2)],
            dst_ref=dst.at[pl.ds(2 * i, 2)],
            send_sem=send.at[i],
            recv_sem=recv.at[i],
            device_id=(dp, to),
            device_id_type=MESH,
        )
        copy.start()
        copies.append(copy)
    for copy in copies:
        copy.wait()


def exchange_states(states):
    return pl.pallas_call(
        states_kernel,
        out_shape=jax.ShapeDtypeStruct((4, DK, DK), f32),
        in_specs=[vspec],
        out_specs=vspec,
        scratch_shapes=[pltpu.SemaphoreType.DMA((2,)), pltpu.SemaphoreType.DMA((2,))],
        compiler_params=pltpu.CompilerParams(collective_id=1, has_side_effects=True),
        name="exchange_states",
    )(states)


def second_kernel(
    meta, states, mixed, halo, grad, weight, summed, q_i, k_i, tile_i, col_i, t_i, w_i, u_i, p_i, a_i,
    b_i, r_i, out_o, dmix_o, edge_o, back_o, taps_o, aux_o, st, rt, gs, cs,
):
    j = meta[0]
    ri, ci = iotas()
    rows = PER * L
    wq = weight[:, pl.ds(pl.multiple_of(j * DK, DK), DK)].astype(f32)
    wk = weight[:, pl.ds(pl.multiple_of((KH + j) * DK, DK), DK)].astype(f32)
    wv = weight[:, pl.ds(pl.multiple_of((2 * KH + 2 * j) * DK, 2 * DK), 2 * DK)].astype(f32)
    taps = jnp.concatenate([wq, wk, wv], axis=1)
    lower = jnp.where(ri >= ci, 1.0, 0.0).astype(f32)

    for h in range(2):
        st[h] = states[h]
        rt[2 * (NB - 1) + h] = states[2 + h]

    def scan(i, carry):
        m = NB - 1 - i
        for h in range(2):
            st[2 * (i + 1) + h] = (
                mm(split(st[2 * i + h]), split(a_i[2 * i + h]), NT) + b_i[2 * i + h]
            )

        @pl.when(m > 0)
        def _():
            for h in range(2):
                rt[2 * (m - 1) + h] = mm(split(rt[2 * m + h]), split(a_i[2 * m + h])) + r_i[2 * m + h]

        return carry

    lax.fori_loop(0, NB, scan, 0)

    gs[rows:, :] = jnp.zeros((8, 4 * DK), f32)
    cs[rows:, :] = jnp.full((8, 8), -2.0, f32)
    taps_o[...] = jnp.zeros((4, 4 * DK), f32)

    def body(step, carry):
        i = NB // PER - 1 - step
        r0 = pl.multiple_of(i * rows, rows)
        cs[0:rows, :] = col_i[pl.ds(pl.multiple_of(r0 + 8, 8), rows), :]
        sm = summed[pl.ds(r0, rows), :]
        sigma = 1.0 / (1.0 + jnp.exp(-sm))
        active = sm * sigma
        d_active = []
        for p in range(PER):
            lo = slice(p * L, (p + 1) * L)
            block = i * PER + p
            rb = pl.multiple_of(r0 + p * L, L)
            tile = tile_i[block]
            columns = cs[lo, :]
            doc_column = columns[:, 4:5]
            doc_before = col_i[pl.ds(pl.multiple_of(rb, 8), 8), :][7:8, 4:5]
            qb, kb = q_i[pl.ds(rb, L), :], k_i[pl.ds(rb, L), :]
            qs, ks = split(qb), split(kb)
            dq = jnp.zeros((L, DK), f32)
            dk = jnp.zeros((L, DK), f32)
            dvs = []
            small = jnp.zeros((L, L), f32)
            for h in range(2):
                n = 2 * block + h
                fade, enter, tail, keep, rate = gates(
                    tile, h, doc_column, tile[4:5, :], doc_before, columns
                )
                state = split(st[n])
                later = rt[n]
                laters = split(later)
                score = p_i[n]
                u = u_i[n] - mm(split(w_i[n]), state, NT)
                us = split(u)
                out = mm(split(enter * qb), state, NT) + mm(split(score), us)
                out_o[pl.ds(rb, L), h * DK : (h + 1) * DK] = out.astype(bf16)
                g = grad[pl.ds(rb, L), h * DK : (h + 1) * DK]
                gs1 = (g,)
                du = mm(split(jnp.transpose(score)), gs1) + mm(split(tail * kb), laters, NT)
                y = mm(split(jnp.transpose(t_i[n])), split(du))
                dv = rate * y
                d_score = mm(gs1, us, NT) * fade
                d_low = jnp.where(ri > ci, mm(split(y), us, NT) * (-rate * fade), 0.0)
                d_scores = split(d_score)
                dq = dq + enter * mm(gs1, state) + mm(d_scores, ks)
                dk = (
                    dk
                    - enter * mm(split(dv), state)
                    + mm(split(d_low + jnp.transpose(d_low)), ks)
                    + mm(split(jnp.transpose(d_score)), qs)
                    + tail * mm(us, laters)
                )
                v = active[lo, (2 + h) * DK : (3 + h) * DK]
                yu = y * u
                d_cum = jnp.sum(out * g.astype(f32) - v * dv, -1, keepdims=True)
                end = jnp.sum(jnp.sum(st[n + 2] * later, -1, keepdims=True), 0, keepdims=True)
                d_cum = d_cum + jnp.where(ri[:, 0:1] == L - 1, end, 0.0)
                d_rate = jnp.sum(yu, -1, keepdims=True) / rate
                small = small + jnp.where(ci == h, d_cum, 0.0) + jnp.where(ci == 2 + h, d_rate, 0.0)
                dvs.append(dv)
            small = jnp.transpose(small)[0:8, :]
            summed_back = exact(small, lower)
            which = lax.broadcasted_iota(jnp.int32, (8, 128), 0)
            aux_o[block] = jnp.where(which < 2, summed_back, small)
            d_active.append((dq, dk, dvs[0], dvs[1]))
        dq, dk, dv0, dv1 = (
            jnp.concatenate([d_active[p][c] for p in range(PER)], axis=0) for c in range(4)
        )
        aq, ak = active[:, :DK], active[:, DK : 2 * DK]
        nq = lax.rsqrt(jnp.sum(aq * aq, -1, keepdims=True) + EPS)
        nk = lax.rsqrt(jnp.sum(ak * ak, -1, keepdims=True) + EPS)
        dq = dq * DK**-0.5
        dq = nq * (dq - aq * (nq * nq * jnp.sum(aq * dq, -1, keepdims=True)))
        dk = nk * (dk - ak * (nk * nk * jnp.sum(ak * dk, -1, keepdims=True)))
        d_all = jnp.concatenate([dq, dk, dv0, dv1], axis=1)
        gs[0:rows, :] = d_all * (sigma * (1.0 + sm * (1.0 - sigma)))

        x = mixed[pl.ds(r0, rows), :].astype(f32)
        doc = cs[0:rows, 4:5]
        d_sum = gs[0:rows, :]
        dx = taps[3:4, :] * d_sum
        parts = [jnp.sum(d_sum * x, 0, keepdims=True)]
        for o in (1, 2, 3):
            moved = jnp.where(cs[o : o + rows, 4:5] == doc, gs[o : o + rows, :], 0.0)
            dx = dx + taps[3 - o : 4 - o, :] * moved
            parts.append(jnp.sum(moved * x, 0, keepdims=True))
        dmix_o[pl.ds(r0, rows), :] = dx.astype(bf16)

        @pl.when(step == 0)
        def _():
            edge_o[...] = dx[rows - 16 :, :]

        taps_o[...] = taps_o[...] + jnp.concatenate(parts[::-1], axis=0)
        gs[rows:, :] = gs[0:8, :]
        cs[rows:, :] = cs[0:8, :]
        return carry

    lax.fori_loop(0, NB // PER, body, 0)

    gs[0:8, :] = jnp.zeros((8, 4 * DK), f32)
    gs[8:16, :] = gs[rows:, :]
    cs[8:16, :] = cs[rows:, :]
    cs[0:8, :] = col_i[0:8, :]
    x = halo[8:16, :].astype(f32)
    dx = jnp.zeros((8, 4 * DK), f32)
    parts = [jnp.zeros((1, 4 * DK), f32)]
    for o in (1, 2, 3):
        moved = jnp.where(cs[o : o + 8, 4:5] == cs[0:8, 4:5], gs[o : o + 8, :], 0.0)
        dx = dx + taps[3 - o : 4 - o, :] * moved
        parts.append(jnp.sum(moved * x, 0, keepdims=True))
    taps_o[...] = taps_o[...] + jnp.concatenate(parts[::-1], axis=0)
    back_o[0:8, :] = jnp.zeros((8, 4 * DK), f32)
    back_o[8:16, :] = dx


def second_phase(meta, states, mixed, halo, grad, weight, kept, interpret=False):
    return pl.pallas_call(
        second_kernel,
        out_shape=(
            jax.ShapeDtypeStruct((QUARTER, 2 * DK), bf16),
            jax.ShapeDtypeStruct((QUARTER, 4 * DK), bf16),
            jax.ShapeDtypeStruct((16, 4 * DK), f32),
            jax.ShapeDtypeStruct((16, 4 * DK), f32),
            jax.ShapeDtypeStruct((4, 4 * DK), f32),
            jax.ShapeDtypeStruct((GROUP, 8, 128), f32),
        ),
        in_specs=[sspec] + [vspec] * 17,
        out_specs=(vspec,) * 6,
        scratch_shapes=[
            VM((2 * NB + 2, DK, DK), f32),
            VM((2 * NB, DK, DK), f32),
            VM((8 + PER * L, 4 * DK), f32),
            VM((8 + PER * L, 8), f32),
        ],
        compiler_params=pltpu.CompilerParams(vmem_limit_bytes=60 * 1024 * 1024),
        name="second_phase",
        interpret=interpret,
    )(meta, states, mixed, halo, grad, weight, *kept)


def tokens_kernel(
    out, dmix, edge, back, taps, aux, o_out, o_mix, o_taps, o_aux, part, total, gathered, edges,
    backs, send, recv, esend, erecv, bsend, brecv, tsend, trecv, gsend, grecv,
):
    dp = lax.axis_index("dp")
    me = lax.axis_index("seq")
    row, j = me // GROUP, lax.rem(me, GROUP)
    base = row * GROUP
    last = GROUP - 1
    before = lax.rem(row + 3, 4) * GROUP
    after = lax.rem(row + 1, 4) * GROUP
    is_last = j == last

    barrier = pltpu.get_barrier_semaphore()
    for s in range(1, GROUP):
        pl.semaphore_signal(
            barrier, inc=1, device_id=(dp, base + lax.rem(j + s, GROUP)), device_id_type=MESH
        )
    for n in range(1, 16):
        pl.semaphore_signal(
            barrier,
            inc=1,
            device_id=(lax.rem(dp + n // 4, 4), lax.rem(me + (n % 4) * GROUP, 4 * GROUP)),
            device_id_type=MESH,
        )

    @pl.when(is_last)
    def _():
        for to in range(GROUP):
            pl.semaphore_signal(barrier, inc=1, device_id=(dp, after + to), device_id_type=MESH)

    pl.semaphore_wait(barrier, GROUP - 1 + 15 + 1)

    def tap_copy(n):
        return pltpu.make_async_remote_copy(
            src_ref=taps.at[:, :],
            dst_ref=part.at[n],
            send_sem=tsend.at[n],
            recv_sem=trecv.at[n],
            device_id=(lax.rem(dp + n // 4, 4), lax.rem(me + (n % 4) * GROUP, 4 * GROUP)),
            device_id_type=MESH,
        )

    for n in range(1, 16):
        tap_copy(n).start()

    back_copy = pltpu.make_async_remote_copy(
        src_ref=back.at[:, :],
        dst_ref=backs.at[j],
        send_sem=bsend,
        recv_sem=brecv.at[j],
        device_id=(dp, before + last),
        device_id_type=MESH,
    )
    back_copy.start()

    def edge_copy():
        return pltpu.make_async_remote_copy(
            src_ref=edge.at[:, :],
            dst_ref=edges.at[j],
            send_sem=esend,
            recv_sem=erecv.at[j],
            device_id=(dp, base + last),
            device_id_type=MESH,
        )

    @pl.when(jnp.logical_not(is_last))
    def _():
        edge_copy().start()

    copies = []
    for s in range(1, GROUP):
        to = lax.rem(j + s, GROUP)
        r = pl.ds(pl.multiple_of(to * 128, 128), 128)
        two = pl.ds(pl.multiple_of(j * 2 * DK, 2 * DK), 2 * DK)
        pairs = (
            (out.at[r, :], o_out.at[:, two]),
            (dmix.at[r, pl.ds(0, DK)], o_mix.at[:, pl.ds(pl.multiple_of(j * DK, DK), DK)]),
            (
                dmix.at[r, pl.ds(DK, DK)],
                o_mix.at[:, pl.ds(pl.multiple_of((KH + j) * DK, DK), DK)],
            ),
            (
                dmix.at[r, pl.ds(2 * DK, 2 * DK)],
                o_mix.at[:, pl.ds(pl.multiple_of((2 * KH + 2 * j) * DK, 2 * DK), 2 * DK)],
            ),
            (aux.at[to], o_aux.at[j]),
        )
        for i, (src, dst) in enumerate(pairs):
            copy = pltpu.make_async_remote_copy(
                src_ref=src,
                dst_ref=dst,
                send_sem=send.at[s, i],
                recv_sem=recv.at[s, i],
                device_id=(dp, base + to),
                device_id_type=MESH,
            )
            copy.start()
            copies.append(copy)

    own = pl.ds(pl.multiple_of(j * 128, 128), 128)
    o_out[:, pl.ds(pl.multiple_of(j * 2 * DK, 2 * DK), 2 * DK)] = out[own, :]
    o_mix[:, pl.ds(pl.multiple_of(j * DK, DK), DK)] = dmix[own, 0:DK]
    o_mix[:, pl.ds(pl.multiple_of((KH + j) * DK, DK), DK)] = dmix[own, DK : 2 * DK]
    o_mix[:, pl.ds(pl.multiple_of((2 * KH + 2 * j) * DK, 2 * DK), 2 * DK)] = dmix[own, 2 * DK :]
    o_aux[j] = aux[j]

    for n in range(1, 16):
        tap_copy(n).wait_recv()
    whole = taps[...]
    for n in range(1, 16):
        whole = whole + part[n]
    total[...] = whole

    def gather_copy(s):
        return pltpu.make_async_remote_copy(
            src_ref=total.at[:, :],
            dst_ref=gathered.at[j],
            send_sem=gsend.at[s],
            recv_sem=grecv.at[s],
            device_id=(dp, base + lax.rem(j + s, GROUP)),
            device_id_type=MESH,
        )

    for s in range(1, GROUP):
        gather_copy(s).start()
    gathered[j] = whole

    for copy in copies:
        copy.wait()

    @pl.when(is_last)
    def _():
        edges[last] = edge[...]
        for src in range(GROUP):
            pltpu.make_async_remote_copy(
                src_ref=back.at[:, :],
                dst_ref=backs.at[src],
                send_sem=bsend,
                recv_sem=brecv.at[src],
                device_id=(dp, before + last),
                device_id_type=MESH,
            ).wait_recv()
        for src in range(GROUP - 1):
            pltpu.make_async_remote_copy(
                src_ref=edge.at[:, :],
                dst_ref=edges.at[src],
                send_sem=esend,
                recv_sem=erecv.at[src],
                device_id=(dp, base),
                device_id_type=MESH,
            ).wait_recv()
        for src in range(GROUP):
            fixed = (edges[src] + backs[src]).astype(bf16)
            o_mix[112:128, src * DK : (src + 1) * DK] = fixed[:, 0:DK]
            o_mix[112:128, (KH + src) * DK : (KH + src + 1) * DK] = fixed[:, DK : 2 * DK]
            o_mix[112:128, (2 * KH + 2 * src) * DK : (2 * KH + 2 * src + 2) * DK] = fixed[:, 2 * DK :]

    for s in range(1, GROUP):
        gather_copy(s).wait()
    for src in range(GROUP):
        o_taps[:, src * DK : (src + 1) * DK] = gathered[src][:, 0:DK]
        o_taps[:, (KH + src) * DK : (KH + src + 1) * DK] = gathered[src][:, DK : 2 * DK]
        o_taps[:, (2 * KH + 2 * src) * DK : (2 * KH + 2 * src + 2) * DK] = gathered[src][:, 2 * DK :]

    for n in range(1, 16):
        tap_copy(n).wait_send()
    back_copy.wait_send()

    @pl.when(jnp.logical_not(is_last))
    def _():
        edge_copy().wait_send()


def to_tokens(out, dmix, edge, back, taps, aux):
    dma = pltpu.SemaphoreType.DMA
    return pl.pallas_call(
        tokens_kernel,
        out_shape=(
            jax.ShapeDtypeStruct((128, 2 * KH * DK), bf16),
            jax.ShapeDtypeStruct((128, 4 * KH * DK), bf16),
            jax.ShapeDtypeStruct((4, 4 * KH * DK), f32),
            jax.ShapeDtypeStruct((GROUP, 8, 128), f32),
        ),
        in_specs=[vspec] * 6,
        out_specs=(vspec,) * 4,
        scratch_shapes=[
            VM((16, 4, 4 * DK), f32),
            VM((4, 4 * DK), f32),
            VM((GROUP, 4, 4 * DK), f32),
            VM((GROUP, 16, 4 * DK), f32),
            VM((GROUP, 16, 4 * DK), f32),
            dma((GROUP, 5)),
            dma((GROUP, 5)),
            dma,
            dma((GROUP,)),
            dma,
            dma((GROUP,)),
            dma((16,)),
            dma((16,)),
            dma((GROUP,)),
            dma((GROUP,)),
        ],
        compiler_params=pltpu.CompilerParams(collective_id=2, has_side_effects=True),
        name="to_tokens",
    )(out, dmix, edge, back, taps, aux)


def small_tiles(log_decay, beta, doc_ids):
    docs = jnp.broadcast_to(doc_ids.astype(f32)[None, None, :], (GROUP, 1, 128))
    return jnp.concatenate(
        [
            log_decay.reshape(GROUP, 2, 128),
            beta.reshape(GROUP, 2, 128),
            docs,
            jnp.zeros((GROUP, 3, 128), f32),
        ],
        axis=1,
    )


def local(mixed, conv_weight, log_decay, beta, doc_ids, out_grad):
    me = lax.axis_index("seq")
    meta = jnp.stack([lax.rem(me, GROUP), (me < GROUP).astype(jnp.int32)]).astype(jnp.int32)
    aux = small_tiles(log_decay[0], beta[0], doc_ids[0])
    rows, grad, aux_all, halo, halo_aux = to_heads(mixed[0], out_grad[0], aux)
    *kept, states = first_phase(meta, rows, halo, grad, aux_all, halo_aux, conv_weight)
    states = exchange_states(states)
    out, dmix, edge, back, taps, d_aux = second_phase(
        meta, states, rows, halo, grad, conv_weight, kept
    )
    out, dmix, taps, d_aux = to_tokens(out, dmix, edge, back, taps, d_aux)
    d_decay = d_aux[:, 0:2, :].reshape(VH, 128)
    d_beta = d_aux[:, 2:4, :].reshape(VH, 128)
    return out[None], dmix[None], taps, d_decay[None], d_beta[None]


def solution(mesh):
    in_specs = (
        P("dp", "seq", None),
        P(),
        P("dp", None, "seq"),
        P("dp", None, "seq"),
        P("dp", "seq"),
        P("dp", "seq", None),
    )
    out_specs = (
        P("dp", "seq", None),
        P("dp", "seq", None),
        P(),
        P("dp", None, "seq"),
        P("dp", None, "seq"),
    )
    return jax.shard_map(local, mesh=mesh, in_specs=in_specs, out_specs=out_specs, check_vma=False)
```

time: 858 us -> 133 us (0.16)
  waiting for transfers between devices: 350 us -> 0 us
  other arithmetic: 208 us -> 2.63 us
  matrix products: 131 us -> 0 us
  Pallas kernels: 0 us -> 123 us
  local copies, waits for them, and re-layouts: 84 us -> 6.33 us
  starting transfers between devices: 59 us -> 0 us
  between operations: 15.6 us -> 0.67 us
    ppermute x19 -> x0, waiting for transfers between devices: 195 us -> none  [passed_along(): return lax.ppermute(array, axis, pairs)]
    another operation x6 -> x1, other arithmetic: 160 us -> 0.58 us  [local(): jnp.stack([lax.rem(me, GROUP), (me < GROUP).astype(jnp.int32)])]
    psum x1 -> x0, waiting for transfers between devices: 155 us -> none  [local(): total_weight = lax.psum(grad_weight, ('dp', 'seq'))]
    dot_general x69 -> x0, matrix products: 124 us -> none  [the longest x16 26.3 us: advance(): jnp.einsum('hij,hjk->hik', transition, carried, precision=highest_precision)]
    pallas_call x0 -> x5, Pallas kernels: none -> 123 us  [the longest x1 31.4 us: to_tokens(): pl.pallas_call(tokens_kernel, out_shape=(jax.ShapeDtypeStruct((128, 2 * K...]
    ppermute x19 -> x0, starting transfers between devices: 58.9 us -> none  [passed_along(): return lax.ppermute(array, axis, pairs)]
    reduce_sum x13 -> x0, other arithmetic: 19.7 us -> none  [the longest x1 9.88 us: prepare(): weight[3 - offset]]
    reshape x10 -> x0, local copies, waits for them, and re-layouts: 14.1 us -> none  [the longest x2 5.17 us: split_blocks(): return array.reshape(blocks, CH, head_count, -1).transpose(0, 2, 1, 3)]
  transfers between devices with their start and end apart: 20 -> 0, of which waited for: 17 -> 0; matrix products, arithmetic and copies ran while one was open for 4% -> 0% of each run, Pallas kernels for 0% -> 0%
where the time goes in v1:
time: 133 us
  Pallas kernels  123 us (92%)
  local copies, waits for them, and re-layouts  6.33 us (5%)
  other arithmetic  2.63 us (2%)
    pallas_call x1, Pallas kernels, to_tokens(): pl.pallas_call(tokens_kernel, out_shape=(jax.ShapeDtypeStruct((128, 2 * K...  31.4 us
    pallas_call x1, Pallas kernels, first_phase(): pl.pallas_call(first_kernel, out_shape=(jax.ShapeDtypeStruct((QUARTER, 4...  29.3 us
    pallas_call x1, Pallas kernels, to_heads(): pl.pallas_call(heads_kernel, out_shape=(jax.ShapeDtypeStruct((QUARTER, 4...  28 us
    pallas_call x1, Pallas kernels, second_phase(): pl.pallas_call(second_kernel, out_shape=(jax.ShapeDtypeStruct((QUARTER, 2...  27.4 us
    pallas_call x1, Pallas kernels, exchange_states(): pl.pallas_call(states_kernel, out_shape=jax.ShapeDtypeStruct((4, DK, DK),...  7.11 us
    unnamed x5, local copies, waits for them, and re-layouts  4.8 us

profile of v1, /device:TPU:1, one launch (start us, length us, event | category | flops | bytes accessed | tf_op | source)
XLA Modules:
  0.0 132.7 jit_solution(7263196527169024485)
XLA Ops:
  0.6 0.6 pad_add_fusion.meta
  1.2 0.7 convert_bitcast_fusion
  1.9 0.1 pad.3.clone
  2.0 1.4 %maximum_maximum_fusion.aux = f32[8,8,128]{2,1,0:T(8,128)} fusion(f32[8,1,128]{2,1,0:T(1,128)S(1)} %broadcast_in_dim.15, f32[8,2,128]{2,1,0:T(2,128)} %bitcast.16, f32[8,2,128]{2,1,0:T(2,128)} %bitcast.17, f32[8]{0:T(128)S(1)} %pad.3.clone), kind=kLoop, calls=%fused_computation | loop fusion | flops 24576 | bytes 53280 | tf_op jit(solution)/shard_map/concatenate | solution.py:769
  3.4 28.0 %to_heads.1 = (bf16[1024,512]{1,0:T(8,128)(2,1)}, bf16[1024,256]{1,0:T(8,128)(2,1)}, f32[8,8,128]{2,1,0:T(8,128)}, bf16[16,512]{1,0:T(8,128)(2,1)}, f32[8,128]{1,0:T(8,128)}) custom-call(bf16[128,4096]{1,0:T(8,128)(2,1)} %bitcast.12, bf16[128,2048]{1,0:T(8,128)(2,1)} %bitcast.14, f32[8,8,128]{2,1,0:T(8,128)} %maximum_maximum_fusion.aux), custom_call_target="tpu_custom_call" | custom-call | tf_op jit(solution)/shard_map/to_heads/pallas_call | solution.py:161
  31.3 29.3 %first_phase.1 = (f32[1024,512]{1,0:T(8,128)}, f32[1024,128]{1,0:T(8,128)}, f32[1024,128]{1,0:T(8,128)}, f32[8,8,128]{2,1,0:T(8,128)}, f32[1032,8]{1,0:T(8,128)}...) custom-call(s32[2]{0:T(128)} %pad_add_fusion.meta, ...), custom_call_target="tpu_custom_call" | custom-call | tf_op jit(solution)/shard_map/first_phase/pallas_call | solution.py:326
  60.6 7.1 %exchange_states.1.states = f32[4,128,128]{2,1,0:T(8,128)} custom-call(f32[4,128,128]{2,1,0:T(8,128)} %get-tuple-element.38.src), custom_call_target="tpu_custom_call" | custom-call | tf_op jit(solution)/shard_map/exchange_states/pallas_call | solution.py:372
  67.7 27.4 %second_phase.1 = (bf16[1024,256]{1,0:T(8,128)(2,1)}, bf16[1024,512]{1,0:T(8,128)(2,1)}, f32[16,512]{1,0:T(8,128)}, f32[16,512]{1,0:T(8,128)}, f32[4,512]{1,0:T(4,128)}, /*index=5*/f32[8,8,128]{2,1,0:T(8,128)}) custom-call(s32[2]{0:T(128)} %pad_add_fusion.meta, f32[4,128,128]{2,1,0:T(8,128)} %exchange_states.1.states, ...), custom_call_target="tpu_custom_call" | custom-call | tf_op jit(solution)/shard_map/second_phase/pallas_call | solution.py:535
  95.1 31.4 %to_tokens.1 = (bf16[128,2048]{1,0:T(8,128)(2,1)}, bf16[128,4096]{1,0:T(8,128)(2,1)}, f32[4,4096]{1,0:T(4,128)}, f32[8,8,128]{2,1,0:T(8,128)}) custom-call(bf16[1024,256]{1,0:T(8,128)(2,1)} %get-tuple-element.51.out, bf16[1024,512]{1,0:T(8,128)(2,1)} %get-tuple-element.52.dmix, f32[16,512]{1,0:T(8,128)} %get-tuple-element.53.edge, ...), custom_call_target="tpu_custom_call" | custom-call | tf_op jit(solution)/shard_map/to_tokens/pallas_call | solution.py:735
  126.5 0.0 copy-start
  126.5 1.4 %fusion = (f32[8,2,128]{2,1,0:T(2,128)}, f32[8,2,128]{2,1,0:T(2,128)}) fusion(f32[8,8,128]{2,1,0:T(8,128)} %get-tuple-element.60), kind=kLoop, calls=%fused_computation.3 | loop fusion | bytes 32768 | tf_op jit(solution)/shard_map/slice | solution.py:792
  127.9 1.9 %copy.14 = bf16[1,128,2048]{2,1,0:T(8,128)(2,1)} copy(bf16[1,128,2048]{2,1,0:T(8,128)(2,1)} %bitcast.15) | data formatting | bytes 1048576
  129.8 2.3 %copy.15 = bf16[1,128,4096]{2,1,0:T(8,128)(2,1)} copy(bf16[1,128,4096]{2,1,0:T(8,128)(2,1)} %bitcast.13) | data formatting | bytes 2097152
  132.1 0.0 copy-done
  132.1 0.6 copy.16
  (2 shorter events, 0.0 us)
Async XLA Ops:
  126.5 5.6 %copy-start = (f32[4,4096]{1,0:T(4,128)S(1)}, f32[4,4096]{1,0:T(4,128)}, u32[]{:S(2)}) copy-start(f32[4,4096]{1,0:T(4,128)} %get-tuple-element.70) | copy-start | bytes 196612

commit v2 on v0

v2 whole, which is shorter than its diff:
```python
import types

import jax
import jax.numpy as jnp
from jax import lax
from jax.experimental import pallas as pl
from jax.experimental.pallas import tpu as pltpu
from jax.sharding import PartitionSpec as P

DK = 128
KH = 8
VH = 16
L = 128
GROUP = 8
CHIPS = GROUP // 2
QUARTER = GROUP * 128
NB = QUARTER // L
PER = 2
ROWS = PER * L
EPS = 1e-6

f32 = jnp.float32
bf16 = jnp.bfloat16
NN = (((1,), (0,)), ((), ()))
NT = (((1,), (1,)), ((), ()))
MESH = pl.DeviceIdType.MESH
VM = pltpu.VMEM
vspec = pl.BlockSpec(memory_space=pltpu.VMEM)


def split(a):
    high = a.astype(bf16)
    return high, (a - high.astype(f32)).astype(bf16)


def stack(*pairs):
    return tuple(jnp.concatenate(x, axis=0) for x in zip(*pairs))


def mm(a, b, dims=NN):
    def dot(p, q):
        return lax.dot_general(p, q, dims, preferred_element_type=f32)

    if len(a) == 1:
        return dot(a[0], b[0]) + dot(a[0], b[1])
    rows = a[0].shape[0]
    both = dot(jnp.concatenate(a, axis=0), b[0])
    return both[:rows] + both[rows:] + dot(a[0], b[1])


def wide(a, b):
    left = jnp.concatenate([a[0], a[1], a[0]], axis=1)
    right = jnp.concatenate([b[0], b[0], b[1]], axis=0)
    return lax.dot_general(left, right, NN, preferred_element_type=f32)


def exact(a, b):
    return lax.dot_general(a, b, NN, preferred_element_type=f32, precision=lax.Precision.HIGHEST)


def iotas(rows=L):
    return (
        lax.broadcasted_iota(jnp.int32, (rows, L), 0),
        lax.broadcasted_iota(jnp.int32, (rows, L), 1),
    )


def invert(lows):
    ri, ci = iotas()
    eye = jnp.where(ri == ci, 1.0, 0.0).astype(f32)
    near = ri // 8 == ci // 8
    d = [jnp.where(near, x, 0.0) for x in lows]
    s1 = [split(x) for x in d]
    d2 = [mm(x, x) for x in s1]
    s2 = [split(x) for x in d2]
    d34 = [mm(stack(x, y), y) for x, y in zip(s1, s2)]
    inverse = [eye - x + y - z[:L] for x, y, z in zip(d, d2, d34)]
    inverse = [x + mm(split(x), split(z[L:])) for x, z in zip(inverse, d34)]
    half, lane = iotas(L // 2)
    size = 8
    while size < L:
        spots = range(0, L, 2 * size)
        mask = lane // size == 2 * (half // size)
        corner = [
            jnp.where(mask, jnp.concatenate([x[r + size : r + 2 * size] for r in spots], 0), 0.0)
            for x in lows
        ]
        inner = [mm(split(c), split(x)) for c, x in zip(corner, inverse)]
        zero = jnp.zeros((size, L), f32)
        spread = [
            jnp.concatenate(
                [p for m in range(len(spots)) for p in (zero, y[m * size : (m + 1) * size])], 0
            )
            for y in inner
        ]
        odd = [jnp.concatenate([x[r + size : r + 2 * size] for r in spots], 0) for x in inverse]
        odd = [x - mm(split(x), split(y)) for x, y in zip(odd, spread)]
        inverse = [
            jnp.concatenate(
                [
                    p
                    for m, r in enumerate(spots)
                    for p in (x[r : r + size], o[m * size : (m + 1) * size])
                ],
                0,
            )
            for x, o in zip(inverse, odd)
        ]
        size *= 2
    return inverse


def gates(tile, h, doc_column, doc_before, columns):
    ri, ci = iotas()
    doc_row = tile[4:5, :]
    cum = columns[:, h : h + 1]
    cum_row = tile[h : h + 1, :]
    doc_last = tile[4:5, L - 1 : L]
    cum_last = tile[h : h + 1, L - 1 : L]
    fade = jnp.where(
        (doc_column == doc_row) & (ri >= ci), jnp.exp(jnp.minimum(cum - cum_row, 0.0)), 0.0
    )
    enter = jnp.where(doc_column == doc_before, jnp.exp(cum), 0.0)
    return fade, enter, cum, cum_row, doc_row, doc_last, cum_last


def prepare_pair(e, i, first, taps):
    ri, ci = iotas()
    r0 = pl.multiple_of(i * ROWS, ROWS)
    e.xs[0:8, :] = e.halo[i][8:16, :].astype(f32)
    e.xs[8:, :] = e.rows[pl.ds(r0, ROWS), :].astype(f32)
    upper = jnp.where(ri <= ci, 1.0, 0.0).astype(f32)
    flat = jnp.concatenate([e.aux[PER * i + p] for p in range(PER)], axis=0)
    sums = exact(flat, upper)
    which = lax.rem(lax.broadcasted_iota(jnp.int32, (PER * 8, 128), 0), 8)
    flat = jnp.where(which < 2, sums, flat)
    tiles = [flat[8 * p : 8 * p + 8] for p in range(PER)]
    edge_columns = jnp.transpose(e.haux[i])[120:128, :]
    at_start = (first + (i == 0).astype(jnp.int32)) == 2
    e.ds[0:8, :] = jnp.where(at_start, -1.0, edge_columns)
    for p in range(PER):
        e.tile[PER * i + p] = tiles[p]
        e.ds[8 + p * L : 8 + (p + 1) * L, :] = jnp.transpose(tiles[p])
    e.col[i] = e.ds[...]
    doc = e.ds[8:, 4:5]
    summed = taps[3:4, :] * e.xs[8:, :]
    for o in (1, 2, 3):
        same = e.ds[8 - o : 8 - o + ROWS, 4:5] == doc
        summed = summed + taps[3 - o : 4 - o, :] * jnp.where(
            same, e.xs[8 - o : 8 - o + ROWS, :], 0.0
        )
    e.summed[pl.ds(r0, ROWS), :] = summed
    active = summed / (1.0 + jnp.exp(-summed))
    q = active[:, :DK]
    k = active[:, DK : 2 * DK]
    q = q * lax.rsqrt(jnp.sum(q * q, -1, keepdims=True) + EPS) * DK**-0.5
    k = k * lax.rsqrt(jnp.sum(k * k, -1, keepdims=True) + EPS)
    e.q[pl.ds(r0, ROWS), :] = q
    e.k[pl.ds(r0, ROWS), :] = k

    chains = []
    for p in range(PER):
        lo = slice(p * L, (p + 1) * L)
        kp, qp = k[lo], q[lo]
        ks = split(kp)
        both = mm(stack(ks, split(qp)), ks, NT)
        inner, score = both[:L], both[L:]
        columns = e.ds[8 + p * L : 8 + (p + 1) * L, :]
        doc_before = e.ds[7 + p * L : 8 + p * L, 4:5]
        turned = jnp.transpose(kp)
        for h in range(2):
            fade, enter, cum, cum_row, doc_row, doc_last, cum_last = gates(
                tiles[p], h, columns[:, 4:5], doc_before, columns
            )
            rate = columns[:, 2 + h : 3 + h]
            tail_row = jnp.where(doc_row == doc_last, jnp.exp(cum_last - cum_row), 0.0)
            keep = jnp.where(doc_last == doc_before, jnp.exp(cum_last), 0.0)
            chains.append(
                dict(
                    n=(PER * i + p) * 2 + h,
                    low=jnp.where(ri > ci, rate * inner * fade, 0.0),
                    left=jnp.concatenate([score * fade, turned * tail_row], axis=0),
                    right=jnp.concatenate(
                        [(rate * enter) * kp, rate * active[lo, (2 + h) * DK : (3 + h) * DK]], axis=1
                    ),
                    eq=enter * qp,
                    keep=keep,
                )
            )
    inverse = invert([c["low"] for c in chains])
    for c, t in zip(chains, inverse):
        n = c["n"]
        ts = split(t)
        ns = split(mm(split(c["left"]), ts))
        e.nh[n] = ns[0]
        e.nl[n] = ns[1]
        big = wide(stack(ts, ns), split(c["right"]))
        ws = split(jnp.concatenate([big[:L, :DK], c["eq"] - big[L : 2 * L, :DK]], axis=0))
        e.wh[n] = ws[0]
        e.wl[n] = ws[1]
        e.u[n] = big[:L, DK:]
        e.o[n] = big[L : 2 * L, DK:]
        a = split(jnp.where(ri == ci, c["keep"], 0.0) - big[2 * L :, :DK])
        e.ah[n] = a[0]
        e.al[n] = a[1]
        e.b[n] = big[2 * L :, DK:]


def backward_terms(e, i):
    for p in range(PER):
        rb = pl.multiple_of(i * ROWS + p * L, L)
        for h in range(2):
            n = (PER * i + p) * 2 + h
            g = e.grad[pl.ds(rb, L), h * DK : (h + 1) * DK]
            turned = jnp.transpose(g.astype(f32)).astype(bf16)
            e.gt[n] = turned
            e.r[n] = mm((turned,), (e.wh[n][L:], e.wl[n][L:]))


def scans(e):
    def step(i, carry):
        m = NB - 1 - i
        for h in range(2):
            n = 2 * i + h
            e.st[n + 2] = mm((e.ah[n], e.al[n]), split(e.st[n])) + e.b[n]
        for h in range(2):
            n = 2 * m + h
            e.rt[n] = mm(split(e.rt[n + 2]), (e.ah[n], e.al[n])) + e.r[n]
        return carry

    lax.fori_loop(0, NB, step, 0)


def finish_pair(e, i, t, taps):
    ri, ci = iotas()
    lower = jnp.where(ri >= ci, 1.0, 0.0).astype(f32)
    r0 = pl.multiple_of(i * ROWS, ROWS)
    e.cs[0 : 8 + ROWS, :] = e.col[i]
    sm = e.summed[pl.ds(r0, ROWS), :]
    sigma = 1.0 / (1.0 + jnp.exp(-sm))
    active = sm * sigma
    pieces = []
    for p in range(PER):
        lo = slice(p * L, (p + 1) * L)
        block = PER * i + p
        rb = pl.multiple_of(r0 + p * L, L)
        tile = e.tile[block]
        columns = e.cs[8 + p * L : 8 + (p + 1) * L, :]
        doc_before = e.cs[7 + p * L : 8 + p * L, 4:5]
        d_score = jnp.zeros((L, L), f32)
        d_low = jnp.zeros((L, L), f32)
        dq = jnp.zeros((L, DK), f32)
        dk = jnp.zeros((L, DK), f32)
        small = jnp.zeros((L, L), f32)
        dvs, ends = [], []
        for h in range(2):
            n = 2 * block + h
            fade, enter, cum, cum_row, doc_row, doc_last, cum_last = gates(
                tile, h, columns[:, 4:5], doc_before, columns
            )
            rate = columns[:, 2 + h : 3 + h]
            tail = jnp.where(columns[:, 4:5] == doc_last, jnp.exp(cum_last - cum), 0.0)
            state = split(e.st[n])
            later = e.rt[n + 2]
            laters = split(later)
            both = mm((e.wh[n], e.wl[n]), state)
            u = e.u[n] - both[:L]
            out = e.o[n] + both[L:]
            e.out[pl.ds(rb, L), h * DK : (h + 1) * DK] = out.astype(bf16)
            g = e.grad[pl.ds(rb, L), h * DK : (h + 1) * DK]
            ns = (e.nh[n], e.nl[n])
            yt = mm((e.gt[n],), (ns[0][:L], ns[1][:L])) + mm(laters, (ns[0][L:], ns[1][L:]))
            y = jnp.transpose(yt)
            ys = split(y)
            us = split(u)
            right = stack(us, state)
            tops = jnp.concatenate([g, ys[0], ys[1]], axis=0)

            def dot(a, b):
                return lax.dot_general(a, b, NT, preferred_element_type=f32)

            res = dot(tops, right[0])
            fine = dot(tops[: 2 * L], right[1])
            gu = res[:L] + fine[:L]
            yu = res[L : 2 * L] + res[2 * L :] + fine[L:]
            d_score = d_score + gu[:, :L] * fade
            d_low = d_low - jnp.where(ri > ci, yu[:, :L] * (rate * fade), 0.0)
            dq = dq + enter * gu[:, L:]
            dk = dk - (enter * rate) * yu[:, L:]
            dv = rate * y
            dvs.append(dv)
            ends.append((us, tail, laters))
            v = active[lo, (2 + h) * DK : (3 + h) * DK]
            d_cum = jnp.sum(out * g.astype(f32) - v * dv, -1, keepdims=True)
            end = jnp.sum(e.st[n + 2] * jnp.transpose(later), -1, keepdims=True)
            end = jnp.sum(end, 0, keepdims=True)
            d_cum = d_cum + jnp.where(ri[:, 0:1] == L - 1, end, 0.0)
            d_rate = jnp.sum(y * u, -1, keepdims=True) / rate
            small = small + jnp.where(ci == h, d_cum, 0.0) + jnp.where(ci == 2 + h, d_rate, 0.0)
        ks = split(e.k[pl.ds(rb, L), :])
        qs = split(e.q[pl.ds(rb, L), :])
        both = mm(split(jnp.concatenate([d_score, d_low + jnp.transpose(d_low)], axis=0)), ks)
        dq = dq + both[:L]
        dk = dk + both[L:] + mm(split(jnp.transpose(d_score)), qs)
        for us, tail, laters in ends:
            dk = dk + tail * mm(us, laters)
        small = jnp.transpose(small)[0:8, :]
        which = lax.broadcasted_iota(jnp.int32, (8, 128), 0)
        e.daux[block] = jnp.where(which < 2, exact(small, lower), small)
        pieces.append((dq, dk, dvs[0], dvs[1]))
    dq, dk, dv0, dv1 = (jnp.concatenate(x, axis=0) for x in zip(*pieces))
    aq, ak = active[:, :DK], active[:, DK : 2 * DK]
    nq = lax.rsqrt(jnp.sum(aq * aq, -1, keepdims=True) + EPS)
    nk = lax.rsqrt(jnp.sum(ak * ak, -1, keepdims=True) + EPS)
    dq = dq * DK**-0.5
    dq = nq * (dq - aq * (nq * nq * jnp.sum(aq * dq, -1, keepdims=True)))
    dk = nk * (dk - ak * (nk * nk * jnp.sum(ak * dk, -1, keepdims=True)))
    d_all = jnp.concatenate([dq, dk, dv0, dv1], axis=1)
    d_sum = d_all * (sigma * (1.0 + sm * (1.0 - sigma)))
    e.gs[8 : 8 + ROWS, :] = d_sum

    x = e.rows[pl.ds(r0, ROWS), :].astype(f32)
    doc = e.cs[8 : 8 + ROWS, 4:5]
    before = e.cs[0:8, 4:5]
    xh = e.halo[i][8:16, :].astype(f32)
    dx = taps[3:4, :] * d_sum
    back = jnp.zeros((8, 4 * DK), f32)
    parts = [jnp.sum(d_sum * x, 0, keepdims=True)]
    for o in (1, 2, 3):
        tap = taps[3 - o : 4 - o, :]
        moved = jnp.where(
            e.cs[8 + o : 8 + o + ROWS, 4:5] == doc, e.gs[8 + o : 8 + o + ROWS, :], 0.0
        )
        dx = dx + tap * moved
        over = jnp.where(e.cs[o : o + 8, 4:5] == before, e.gs[o : o + 8, :], 0.0)
        back = back + tap * over
        parts.append(
            jnp.sum(moved * x, 0, keepdims=True) + jnp.sum(over * xh, 0, keepdims=True)
        )
    e.dmix[pl.ds(r0, ROWS), :] = dx.astype(bf16)
    e.edge[t] = dx[ROWS - 8 :, :]
    e.back[t] = back
    e.taps[...] = e.taps[...] + jnp.concatenate(parts[::-1], axis=0)


def start_finish(e):
    e.gs[0:8, :] = jnp.zeros((8, 4 * DK), f32)
    e.gs[8 + ROWS :, :] = jnp.zeros((8, 4 * DK), f32)
    e.cs[8 + ROWS :, :] = jnp.full((8, 8), -2.0, f32)
    e.taps[...] = jnp.zeros((4, 4 * DK), f32)


def head_taps(weight, j):
    wq = weight[:, pl.ds(pl.multiple_of(j * DK, DK), DK)]
    wk = weight[:, pl.ds(pl.multiple_of((KH + j) * DK, DK), DK)]
    wv = weight[:, pl.ds(pl.multiple_of((2 * KH + 2 * j) * DK, 2 * DK), 2 * DK)]
    return jnp.concatenate([wq.astype(f32), wk.astype(f32), wv.astype(f32)], axis=1)


SQ = (2 * NB, DK, DK)
SCRATCH = dict(
    rows=((QUARTER, 4 * DK), bf16),
    grad=((QUARTER, 2 * DK), bf16),
    aux=((GROUP, 8, 128), f32),
    halo=((CHIPS, 16, 4 * DK), bf16),
    haux=((CHIPS, 8, 128), f32),
    xs=((8 + ROWS, 4 * DK), f32),
    ds=((8 + ROWS, 8), f32),
    tile=((NB, 8, 128), f32),
    col=((CHIPS, 8 + ROWS, 8), f32),
    summed=((QUARTER, 4 * DK), f32),
    q=((QUARTER, DK), f32),
    k=((QUARTER, DK), f32),
    nh=((2 * NB, 2 * L, L), bf16),
    nl=((2 * NB, 2 * L, L), bf16),
    wh=((2 * NB, 2 * L, DK), bf16),
    wl=((2 * NB, 2 * L, DK), bf16),
    ah=(SQ, bf16),
    al=(SQ, bf16),
    u=(SQ, f32),
    o=(SQ, f32),
    b=(SQ, f32),
    r=(SQ, f32),
    gt=(SQ, bf16),
    st=((2 * NB + 2, DK, DK), f32),
    rt=((2 * NB + 2, DK, DK), f32),
    cs=((16 + ROWS, 8), f32),
    gs=((16 + ROWS, 4 * DK), f32),
    out=((QUARTER, 2 * DK), bf16),
    dmix=((QUARTER, 4 * DK), bf16),
    edge=((CHIPS, 8, 4 * DK), f32),
    back=((CHIPS, 8, 4 * DK), f32),
    taps=((4, 4 * DK), f32),
    daux=((GROUP, 8, 128), f32),
)


ARGS = ("mixed", "weight", "decay", "rate", "docs", "grad_in")
OUTS = ("o_out", "o_mix", "o_taps", "o_decay", "o_rate")
EXTRA = dict(
    aux_own=((GROUP, 8, 128), f32),
    arrived=((4, DK, DK), f32),
    edges=((GROUP, 8, 4 * DK), f32),
    backs=((GROUP, 8, 4 * DK), f32),
    part=((16, 4, 4 * DK), f32),
    total=((4, 4 * DK), f32),
    gathered=((GROUP, 4, 4 * DK), f32),
    daux_in=((GROUP, 8, 128), f32),
)
SEMS = dict(
    asend=(GROUP, 5),
    arecv=(GROUP, 5),
    hsend=(GROUP, 4),
    hrecv=(CHIPS, 4),
    ssend=(2,),
    srecv=(2,),
    bsend=(CHIPS,),
    brecv=(GROUP,),
    esend=(CHIPS,),
    erecv=(GROUP,),
    fsend=(GROUP, 5),
    frecv=(GROUP, 5),
    tsend=(16,),
    trecv=(16,),
    gsend=(GROUP,),
    grecv=(GROUP,),
)
NAMES = ARGS + OUTS + tuple(SCRATCH) + tuple(EXTRA) + tuple(SEMS)


def head_columns(to):
    return (
        pl.ds(pl.multiple_of(to * DK, DK), DK),
        pl.ds(pl.multiple_of((KH + to) * DK, DK), DK),
        pl.ds(pl.multiple_of((2 * KH + 2 * to) * DK, 2 * DK), 2 * DK),
    )


OWN = (pl.ds(0, DK), pl.ds(DK, DK), pl.ds(2 * DK, 2 * DK))


def two_columns(to):
    return pl.ds(pl.multiple_of(to * 2 * DK, 2 * DK), 2 * DK)


def place(j):
    return pl.ds(pl.multiple_of(j * 128, 128), 128)


def layer_kernel(*refs):
    e = types.SimpleNamespace(**dict(zip(NAMES, refs)))
    dp = lax.axis_index("dp")
    me = lax.axis_index("seq")
    row, j = me // GROUP, lax.rem(me, GROUP)
    y, c = j // 2, lax.rem(j, 2)
    base = row * GROUP
    last = GROUP - 1
    before = lax.rem(row + 3, 4) * GROUP
    after = lax.rem(row + 1, 4) * GROUP
    is_last = j == last
    first = (row == 0).astype(jnp.int32)

    def remote(src, dst, send, recv, seq, slab=None):
        return pltpu.make_async_remote_copy(
            src_ref=src,
            dst_ref=dst,
            send_sem=send,
            recv_sem=recv,
            device_id=(dp if slab is None else slab, seq),
            device_id_type=MESH,
        )

    def peer(dy, dc):
        return 2 * lax.rem(y + dy, CHIPS) + lax.rem(c + dc, 2)

    def plane(n):
        return lax.rem(dp + n // 4, 4), lax.rem(me + (n % 4) * GROUP, 4 * GROUP)

    barrier = pltpu.get_barrier_semaphore()

    def greet(slab, seq):
        pl.semaphore_signal(barrier, inc=1, device_id=(slab, seq), device_id_type=MESH)

    for s in range(1, GROUP):
        greet(dp, base + lax.rem(j + s, GROUP))
    for n in range(1, 16):
        greet(*plane(n))
    greet(dp, before + last)

    @pl.when(is_last)
    def _():
        for to in range(GROUP):
            greet(dp, after + to)

    docs = e.docs[...].astype(f32)
    for to in range(GROUP):
        e.aux_own[to] = jnp.concatenate(
            [
                e.decay[2 * to : 2 * to + 2, :],
                e.rate[2 * to : 2 * to + 2, :],
                docs,
                jnp.zeros((3, 128), f32),
            ],
            axis=0,
        )
    taps = head_taps(e.weight, j)
    pl.semaphore_wait(barrier, jnp.where(is_last, GROUP - 1 + 15 + 1 + GROUP, GROUP - 1 + 15 + 1))

    slot = lax.rem(y + 1, CHIPS)
    inside = y < CHIPS - 1
    there = jnp.where(inside, base, after)

    def halo_copies(to, at, group):
        own = head_columns(to)
        r = pl.ds(112, 16)
        pairs = [(e.mixed.at[r, own[n]], e.halo.at[at, :, OWN[n]]) for n in range(3)]
        pairs.append((e.aux_own.at[to], e.haux.at[at]))
        return [
            remote(src, dst, e.hsend.at[to, n], e.hrecv.at[at, n], group + to)
            for n, (src, dst) in enumerate(pairs)
        ]

    @pl.when(c == 1)
    def _():
        for to in range(GROUP):

            @pl.when(jnp.logical_not(inside) | (j != to))
            def _():
                for copy in halo_copies(to, slot, there):
                    copy.start()

        @pl.when(inside)
        def _():
            own = head_columns(j)
            for n in range(3):
                e.halo[slot, :, OWN[n]] = e.mixed[112:128, own[n]]
            e.haux[slot] = e.aux_own[j]

    def dy_of(t):
        return t + t // 2 - 2 * (t // 3)

    def head_copy(t, dc, n):
        to = peer(dy_of(t), dc)
        own = head_columns(to)
        at = place(j)
        src, dst = (
            (e.mixed.at[:, own[0]], e.rows.at[at, OWN[0]]),
            (e.mixed.at[:, own[1]], e.rows.at[at, OWN[1]]),
            (e.mixed.at[:, own[2]], e.rows.at[at, OWN[2]]),
            (e.aux_own.at[to], e.aux.at[j]),
            (e.grad_in.at[:, two_columns(to)], e.grad.at[at, :]),
        )[n]
        k = 2 * t + dc
        return remote(src, dst, e.asend.at[k, n], e.arecv.at[k, n], base + to)

    steps = [(t, dc) for t in range(CHIPS) for dc in range(2) if (t, dc) != (0, 0)]
    for t, dc in steps:
        for n in range(4):
            head_copy(t, dc, n).start()
    for t, dc in steps:
        head_copy(t, dc, 4).start()

    own = head_columns(j)
    for n in range(3):
        e.rows[place(j), OWN[n]] = e.mixed[:, own[n]]
    e.aux[j] = e.aux_own[j]
    e.grad[place(j), :] = e.grad_in[:, two_columns(j)]

    def pair_of(t):
        return lax.rem(y + CHIPS - dy_of(t), CHIPS)

    def prepare(t, carry):
        i = pair_of(t)

        @pl.when(t > 0)
        def _():
            for n in range(4):
                head_copy(t, 0, n).wait_recv()

        for n in range(4):
            head_copy(t, 1, n).wait_recv()

        @pl.when((i == 0) | (2 * i - 1 != j))
        def _():
            for copy in halo_copies(0, i, base):
                copy.wait_recv()

        prepare_pair(e, i, first, taps)
        return carry

    lax.fori_loop(0, CHIPS, prepare, 0)

    def turn(t, carry):
        @pl.when(t > 0)
        def _():
            head_copy(t, 0, 4).wait_recv()

        head_copy(t, 1, 4).wait_recv()
        backward_terms(e, pair_of(t))
        return carry

    lax.fori_loop(0, CHIPS, turn, 0)

    zero = jnp.zeros((2, DK, DK), f32)
    e.st[0:2] = zero
    e.rt[2 * NB :] = zero
    scans(e)
    start_finish(e)
    hops = (
        remote(
            e.st.at[pl.ds(2 * NB, 2)],
            e.arrived.at[pl.ds(0, 2)],
            e.ssend.at[0],
            e.srecv.at[0],
            lax.rem(me + GROUP, 4 * GROUP),
        ),
        remote(
            e.rt.at[pl.ds(0, 2)],
            e.arrived.at[pl.ds(2, 2)],
            e.ssend.at[1],
            e.srecv.at[1],
            lax.rem(me + 3 * GROUP, 4 * GROUP),
        ),
    )
    for copy in hops:
        copy.start()
    for t, dc in steps:
        for n in range(5):
            head_copy(t, dc, n).wait_send()

    @pl.when(c == 1)
    def _():
        for to in range(GROUP):

            @pl.when(jnp.logical_not(inside) | (j != to))
            def _():
                for copy in halo_copies(to, slot, there):
                    copy.wait_send()

    for copy in hops:
        copy.wait()
    e.st[0:2] = e.arrived[0:2]
    e.rt[2 * NB :] = e.arrived[2:4]
    scans(e)

    def token_copies(t, dc):
        to = peer(t + 1, dc)
        r = place(to)
        own = head_columns(j)
        pairs = [(e.out.at[r, :], e.o_out.at[:, two_columns(j)])]
        pairs += [(e.dmix.at[r, OWN[n]], e.o_mix.at[:, own[n]]) for n in range(3)]
        pairs.append((e.daux.at[to], e.daux_in.at[j]))
        k = 2 * t + dc
        return [
            remote(src, dst, e.fsend.at[k, n], e.frecv.at[k, n], base + to)
            for n, (src, dst) in enumerate(pairs)
        ]

    def edge_copy(i, at):
        return remote(
            e.edge.at[at], e.edges.at[j], e.esend.at[at], e.erecv.at[j], base + 2 * i + 1
        )

    def back_copy(i, at):
        to = jnp.where(i == 0, before + last, base + 2 * i - 1)
        return remote(e.back.at[at], e.backs.at[j], e.bsend.at[at], e.brecv.at[j], to)

    def finish(t, carry):
        i = lax.rem(y + t + 1, CHIPS)
        finish_pair(e, i, t, taps)

        @pl.when(t < CHIPS - 1)
        def _():
            for copy in token_copies(t, 0):
                copy.start()

        for copy in token_copies(t, 1):
            copy.start()

        @pl.when(2 * i + 1 == j)
        def _():
            e.edges[j] = e.edge[t]

        @pl.when(2 * i + 1 != j)
        def _():
            edge_copy(i, t).start()

        @pl.when((i > 0) & (2 * i - 1 == j))
        def _():
            e.backs[j] = e.back[t]

        @pl.when((i == 0) | (2 * i - 1 != j))
        def _():
            back_copy(i, t).start()

        return carry

    lax.fori_loop(0, CHIPS, finish, 0)

    spot = 4 * dp + row

    def tap_copy(n):
        slab, seq = plane(n)
        return remote(e.taps.at[:, :], e.part.at[spot], e.tsend.at[n], e.trecv.at[n], seq, slab)

    for n in range(1, 16):
        tap_copy(n).start()

    own = head_columns(j)
    e.o_out[:, two_columns(j)] = e.out[place(j), :]
    for n in range(3):
        e.o_mix[:, own[n]] = e.dmix[place(j), OWN[n]]
    e.daux_in[j] = e.daux[j]

    for n in range(1, 16):
        tap_copy(n).wait_recv()
    e.part[spot] = e.taps[...]
    whole = e.part[0]
    for n in range(1, 16):
        whole = whole + e.part[n]
    e.total[...] = whole
    e.gathered[j] = whole

    def gather_copy(s):
        return remote(
            e.total.at[:, :],
            e.gathered.at[j],
            e.gsend.at[s],
            e.grecv.at[s],
            base + lax.rem(j + s, GROUP),
        )

    for s in range(1, GROUP):
        gather_copy(s).start()

    for t in range(CHIPS):
        for dc in range(2):
            if (t, dc) != (CHIPS - 1, 0):
                for copy in token_copies(t, dc):
                    copy.wait()

    @pl.when(c == 1)
    def _():
        for src in range(GROUP):

            def edge_from():
                return remote(
                    e.edge.at[0], e.edges.at[src], e.esend.at[0], e.erecv.at[src], base + last
                )

            def back_from():
                return remote(
                    e.back.at[0], e.backs.at[src], e.bsend.at[0], e.brecv.at[src], base + last
                )

            @pl.when(j != src)
            def _():
                edge_from().wait_recv()

            @pl.when(jnp.logical_not(inside) | (j != src))
            def _():
                back_from().wait_recv()

        for src in range(GROUP):
            fixed = e.edges[src] + e.backs[src]
            spots = (
                (src * DK, DK, 0),
                ((KH + src) * DK, DK, DK),
                ((2 * KH + 2 * src) * DK, 2 * DK, 2 * DK),
            )
            for at, width, own_at in spots:
                old = e.o_mix[112:128, at : at + width].astype(f32)
                new = jnp.concatenate([old[0:8], fixed[:, own_at : own_at + width]], axis=0)
                e.o_mix[112:128, at : at + width] = new.astype(bf16)

    for src in range(GROUP):
        e.o_decay[2 * src : 2 * src + 2, :] = e.daux_in[src][0:2, :]
        e.o_rate[2 * src : 2 * src + 2, :] = e.daux_in[src][2:4, :]

    for s in range(1, GROUP):
        gather_copy(s).wait()
    for src in range(GROUP):
        got = e.gathered[src]
        e.o_taps[:, src * DK : (src + 1) * DK] = got[:, 0:DK]
        e.o_taps[:, (KH + src) * DK : (KH + src + 1) * DK] = got[:, DK : 2 * DK]
        e.o_taps[:, (2 * KH + 2 * src) * DK : (2 * KH + 2 * src + 2) * DK] = got[:, 2 * DK :]

    for n in range(1, 16):
        tap_copy(n).wait_send()
    for t in range(CHIPS):
        i = lax.rem(y + t + 1, CHIPS)

        @pl.when(2 * i + 1 != j)
        def _():
            edge_copy(i, t).wait_send()

        @pl.when((i == 0) | (2 * i - 1 != j))
        def _():
            back_copy(i, t).wait_send()


def layer(*args):
    scratch = [VM(*x) for x in SCRATCH.values()] + [VM(*x) for x in EXTRA.values()]
    return pl.pallas_call(
        layer_kernel,
        out_shape=(
            jax.ShapeDtypeStruct((128, 2 * KH * DK), bf16),
            jax.ShapeDtypeStruct((128, 4 * KH * DK), bf16),
            jax.ShapeDtypeStruct((4, 4 * KH * DK), f32),
            jax.ShapeDtypeStruct((VH, 128), f32),
            jax.ShapeDtypeStruct((VH, 128), f32),
        ),
        in_specs=[vspec] * len(ARGS),
        out_specs=(vspec,) * len(OUTS),
        scratch_shapes=scratch + [pltpu.SemaphoreType.DMA(x) for x in SEMS.values()],
        compiler_params=pltpu.CompilerParams(
            collective_id=0, has_side_effects=True, vmem_limit_bytes=60 * 1024 * 1024
        ),
        name="layer",
    )(*args)


def local(mixed, conv_weight, log_decay, beta, doc_ids, out_grad):
    out, dmix, taps, d_decay, d_beta = layer(
        mixed[0], conv_weight, log_decay[0], beta[0], doc_ids, out_grad[0]
    )
    return out[None], dmix[None], taps, d_decay[None], d_beta[None]


def solution(mesh):
    in_specs = (
        P("dp", "seq", None),
        P(),
        P("dp", None, "seq"),
        P("dp", None, "seq"),
        P("dp", "seq"),
        P("dp", "seq", None),
    )
    out_specs = (
        P("dp", "seq", None),
        P("dp", "seq", None),
        P(),
        P("dp", None, "seq"),
        P("dp", None, "seq"),
    )
    return jax.shard_map(local, mesh=mesh, in_specs=in_specs, out_specs=out_specs, check_vma=False)
```

time: 858 us -> 77.1 us (0.09)
  waiting for transfers between devices: 350 us -> 0 us
  other arithmetic: 208 us -> 0 us
  matrix products: 131 us -> 0 us
  local copies, waits for them, and re-layouts: 84 us -> 4.94 us
  Pallas kernels: 0 us -> 70.9 us
  starting transfers between devices: 59 us -> 0 us
  between operations: 15.6 us -> 0.65 us
    ppermute x19 -> x0, waiting for transfers between devices: 195 us -> none  [passed_along(): return lax.ppermute(array, axis, pairs)]
    another operation x6 -> x0, other arithmetic: 160 us -> none  [the longest x4 159 us: prepare(): jax.scipy.linalg.solve_triangular(triangle, right_side, lower=True, unit_...]
    psum x1 -> x0, waiting for transfers between devices: 155 us -> none  [local(): total_weight = lax.psum(grad_weight, ('dp', 'seq'))]
    dot_general x69 -> x0, matrix products: 124 us -> none  [the longest x16 26.3 us: advance(): jnp.einsum('hij,hjk->hik', transition, carried, precision=highest_precision)]
    pallas_call x0 -> x1, Pallas kernels: none -> 70.9 us  [layer(): pl.pallas_call(layer_kernel, out_shape=(jax.ShapeDtypeStruct((128, 2 * KH...]
    ppermute x19 -> x0, starting transfers between devices: 58.9 us -> none  [passed_along(): return lax.ppermute(array, axis, pairs)]
    reduce_sum x13 -> x0, other arithmetic: 19.7 us -> none  [the longest x1 9.88 us: prepare(): weight[3 - offset]]
    reshape x10 -> x0, local copies, waits for them, and re-layouts: 14.1 us -> none  [the longest x2 5.17 us: split_blocks(): return array.reshape(blocks, CH, head_count, -1).transpose(0, 2, 1, 3)]
  transfers between devices with their start and end apart: 20 -> 0, of which waited for: 17 -> 0; matrix products, arithmetic and copies ran while one was open for 4% -> 0% of each run, Pallas kernels for 0% -> 0%
where the time goes in v2:
time: 77.1 us; the launch traced here: 76.5 us
  Pallas kernels  70.9 us (92%)
  local copies, waits for them, and re-layouts  4.94 us (6%)
    pallas_call x1, Pallas kernels, layer(): pl.pallas_call(layer_kernel, out_shape=(jax.ShapeDtypeStruct((128, 2 * KH...  70.9 us
    unnamed x13, local copies, waits for them, and re-layouts  4.94 us

profile of v2, /device:TPU:1, one launch (start us, length us, event | category | flops | bytes accessed | tf_op | source)
XLA Modules:
  0.0 76.5 jit_solution(8715762171620740332)
XLA Ops:
  0.6 70.9 %layer.1 = (bf16[128,2048]{1,0:T(8,128)(2,1)}, bf16[128,4096]{1,0:T(8,128)(2,1)}, f32[4,4096]{1,0:T(4,128)}, f32[16,128]{1,0:T(8,128)}, f32[16,128]{1,0:T(8,128)}) custom-call(bf16[128,4096]{1,0:T(8,128)(2,1)} %bitcast.8, bf16[4,4096]{1,0:T(4,128)(2,1)} %refs_1_.1, f32[16,128]{1,0:T(8,128)} %bitcast.12, f32[16,128]{1,0:T(8,128)} %bitcast.13, ...), custom_call_target="tpu_custom_call" | custom-call | tf_op jit(solution)/shard_map/layer/pallas_call | solution.py:804
  71.6 0.0 copy-start
  71.6 2.0 %copy.16 = bf16[1,128,2048]{2,1,0:T(8,128)(2,1)} copy(bf16[1,128,2048]{2,1,0:T(8,128)(2,1)} %bitcast.11) | data formatting | bytes 1048576
  73.6 0.0 copy-done
  73.6 0.0 copy-start.1
  73.6 1.0 %copy.17 = bf16[1,128,4096]{2,1,0:T(8,128)(2,1)} copy(bf16[1,128,4096]{2,1,0:T(8,128)(2,1)S(1)} %bitcast.9) | data formatting | bytes 2097152
  74.5 0.0 copy-done.1
  74.5 0.0 copy-start.3
  74.5 0.6 copy.18
  75.2 0.1 copy-done.3
  75.2 0.0 copy-start.2
  75.2 0.6 copy.19
  75.8 0.1 copy-done.2
  75.9 0.6 copy.20
Async XLA Ops:
  71.6 2.0 %copy-start = (bf16[128,4096]{1,0:T(8,128)(2,1)S(1)}, bf16[128,4096]{1,0:T(8,128)(2,1)}, u32[]{:S(2)}) copy-start(bf16[128,4096]{1,0:T(8,128)(2,1)} %get-tuple-element.11) | copy-start | bytes 3145732
  73.6 1.0 %copy-start.1 = (f32[4,4096]{1,0:T(4,128)S(1)}, f32[4,4096]{1,0:T(4,128)}, u32[]{:S(2)}) copy-start(f32[4,4096]{1,0:T(4,128)} %get-tuple-element.22) | copy-start | bytes 196612
  74.5 0.7 copy-start.3
  75.2 0.7 copy-start.2

commit v3 on v2

--- a/solution.py
+++ b/solution.py
@@ -217,18 +217,60 @@
             e.r[n] = mm((turned,), (e.wh[n][L:], e.wl[n][L:]))
 
 
-def scans(e):
+def scan_forward(e):
+    ri, ci = iotas()
+    eye = jnp.where(ri == ci, 1.0, 0.0).astype(f32)
+    for h in range(2):
+        e.st[h] = jnp.zeros((DK, DK), f32)
+        e.pi[h] = eye
+
     def step(i, carry):
-        m = NB - 1 - i
         for h in range(2):
             n = 2 * i + h
-            e.st[n + 2] = mm((e.ah[n], e.al[n]), split(e.st[n])) + e.b[n]
+            got = wide((e.ah[n], e.al[n]), split(jnp.concatenate([e.st[n], e.pi[n]], axis=1)))
+            e.st[n + 2] = got[:, :DK] + e.b[n]
+            e.pi[n + 2] = got[:, DK:]
+        return carry
+
+    lax.fori_loop(0, NB, step, 0)
+
+
+def scan_backward(e):
+    ri, ci = iotas()
+    eye = jnp.where(ri == ci, 1.0, 0.0).astype(f32)
+    for h in range(2):
+        e.rt[2 * NB + h] = jnp.zeros((DK, DK), f32)
+        e.ps[2 * NB + h] = eye
+
+    def step(i, carry):
         for h in range(2):
-            n = 2 * m + h
-            e.rt[n] = mm(split(e.rt[n + 2]), (e.ah[n], e.al[n])) + e.r[n]
+            n = 2 * (NB - 1 - i) + h
+            got = mm(split(jnp.concatenate([e.rt[n + 2], e.ps[n + 2]], axis=0)), (e.ah[n], e.al[n]))
+            e.rt[n] = got[:DK] + e.r[n]
+            e.ps[n] = got[DK:]
         return carry
 
     lax.fori_loop(0, NB, step, 0)
+
+
+def last_state(e):
+    for h in range(2):
+        e.st[2 * NB + h] = e.st[2 * NB + h] + mm(split(e.pi[2 * NB + h]), split(e.arrived[h]))
+
+
+def read_pair(e, i):
+    entered = [split(e.arrived[h]) for h in range(2)]
+    for p in range(PER):
+        rb = pl.multiple_of(i * ROWS + p * L, L)
+        for h in range(2):
+            n = 2 * (PER * i + p) + h
+            state = e.st[n] + mm(split(e.pi[n]), entered[h])
+            e.st[n] = state
+            both = mm((e.wh[n], e.wl[n]), split(state))
+            e.u[n] = e.u[n] - both[:L]
+            out = e.o[n] + both[L:]
+            e.o[n] = out
+            e.out[pl.ds(rb, L), h * DK : (h + 1) * DK] = out.astype(bf16)
 
 
 def finish_pair(e, i, t, taps):
@@ -239,6 +281,7 @@
     sm = e.summed[pl.ds(r0, ROWS), :]
     sigma = 1.0 / (1.0 + jnp.exp(-sm))
     active = sm * sigma
+    left = [split(e.arrived[2 + h]) for h in range(2)]
     pieces = []
     for p in range(PER):
         lo = slice(p * L, (p + 1) * L)
@@ -261,12 +304,10 @@
             rate = columns[:, 2 + h : 3 + h]
             tail = jnp.where(columns[:, 4:5] == doc_last, jnp.exp(cum_last - cum), 0.0)
             state = split(e.st[n])
-            later = e.rt[n + 2]
+            later = e.rt[n + 2] + mm(left[h], split(e.ps[n + 2]))
             laters = split(later)
-            both = mm((e.wh[n], e.wl[n]), state)
-            u = e.u[n] - both[:L]
-            out = e.o[n] + both[L:]
-            e.out[pl.ds(rb, L), h * DK : (h + 1) * DK] = out.astype(bf16)
+            u = e.u[n]
+            out = e.o[n]
             g = e.grad[pl.ds(rb, L), h * DK : (h + 1) * DK]
             ns = (e.nh[n], e.nl[n])
             yt = mm((e.gt[n],), (ns[0][:L], ns[1][:L])) + mm(laters, (ns[0][L:], ns[1][L:]))
@@ -337,8 +378,10 @@
         parts.append(
             jnp.sum(moved * x, 0, keepdims=True) + jnp.sum(over * xh, 0, keepdims=True)
         )
-    e.dmix[pl.ds(r0, ROWS), :] = dx.astype(bf16)
-    e.edge[t] = dx[ROWS - 8 :, :]
+    rest = jnp.where((t > 0) & (i < CHIPS - 1), e.back[lax.rem(t + 3, CHIPS)], 0.0)
+    edge = dx[ROWS - 8 :, :] + rest
+    e.dmix[pl.ds(r0, ROWS), :] = jnp.concatenate([dx[: ROWS - 8, :], edge], axis=0).astype(bf16)
+    e.edge[t] = edge
     e.back[t] = back
     e.taps[...] = e.taps[...] + jnp.concatenate(parts[::-1], axis=0)
 
@@ -348,6 +391,7 @@
     e.gs[8 + ROWS :, :] = jnp.zeros((8, 4 * DK), f32)
     e.cs[8 + ROWS :, :] = jnp.full((8, 8), -2.0, f32)
     e.taps[...] = jnp.zeros((4, 4 * DK), f32)
+    e.back[...] = jnp.zeros((CHIPS, 8, 4 * DK), f32)
 
 
 def head_taps(weight, j):
@@ -384,6 +428,9 @@
     gt=(SQ, bf16),
     st=((2 * NB + 2, DK, DK), f32),
     rt=((2 * NB + 2, DK, DK), f32),
+    pi=((2 * NB + 2, DK, DK), f32),
+    ps=((2 * NB + 2, DK, DK), f32),
+    arrived=((4, DK, DK), f32),
     cs=((16 + ROWS, 8), f32),
     gs=((16 + ROWS, 4 * DK), f32),
     out=((QUARTER, 2 * DK), bf16),
@@ -399,7 +446,6 @@
 OUTS = ("o_out", "o_mix", "o_taps", "o_decay", "o_rate")
 EXTRA = dict(
     aux_own=((GROUP, 8, 128), f32),
-    arrived=((4, DK, DK), f32),
     edges=((GROUP, 8, 4 * DK), f32),
     backs=((GROUP, 8, 4 * DK), f32),
     part=((16, 4, 4 * DK), f32),
@@ -590,6 +636,15 @@
 
     lax.fori_loop(0, CHIPS, prepare, 0)
 
+    def hop(n, src, to):
+        return remote(src, e.arrived.at[pl.ds(2 * n, 2)], e.ssend.at[n], e.srecv.at[n], to)
+
+    forth = hop(0, e.st.at[pl.ds(2 * NB, 2)], lax.rem(me + GROUP, 4 * GROUP))
+    back = hop(1, e.rt.at[pl.ds(0, 2)], lax.rem(me + 3 * GROUP, 4 * GROUP))
+    scan_forward(e)
+    start_finish(e)
+    forth.start()
+
     def turn(t, carry):
         @pl.when(t > 0)
         def _():
@@ -600,30 +655,7 @@
         return carry
 
     lax.fori_loop(0, CHIPS, turn, 0)
-
-    zero = jnp.zeros((2, DK, DK), f32)
-    e.st[0:2] = zero
-    e.rt[2 * NB :] = zero
-    scans(e)
-    start_finish(e)
-    hops = (
-        remote(
-            e.st.at[pl.ds(2 * NB, 2)],
-            e.arrived.at[pl.ds(0, 2)],
-            e.ssend.at[0],
-            e.srecv.at[0],
-            lax.rem(me + GROUP, 4 * GROUP),
-        ),
-        remote(
-            e.rt.at[pl.ds(0, 2)],
-            e.arrived.at[pl.ds(2, 2)],
-            e.ssend.at[1],
-            e.srecv.at[1],
-            lax.rem(me + 3 * GROUP, 4 * GROUP),
-        ),
-    )
-    for copy in hops:
-        copy.start()
+    scan_backward(e)
     for t, dc in steps:
         for n in range(5):
             head_copy(t, dc, n).wait_send()
@@ -637,59 +669,76 @@
                 for copy in halo_copies(to, slot, there):
                     copy.wait_send()
 
-    for copy in hops:
-        copy.wait()
-    e.st[0:2] = e.arrived[0:2]
-    e.rt[2 * NB :] = e.arrived[2:4]
-    scans(e)
-
-    def token_copies(t, dc):
-        to = peer(t + 1, dc)
+    back.start()
+    forth.wait()
+    last_state(e)
+
+    def token_copy(t, dc, n):
+        to = peer(CHIPS - 1 - t, dc)
         r = place(to)
         own = head_columns(j)
-        pairs = [(e.out.at[r, :], e.o_out.at[:, two_columns(j)])]
-        pairs += [(e.dmix.at[r, OWN[n]], e.o_mix.at[:, own[n]]) for n in range(3)]
-        pairs.append((e.daux.at[to], e.daux_in.at[j]))
+        src, dst = (
+            (e.out.at[r, :], e.o_out.at[:, two_columns(j)]),
+            (e.dmix.at[r, OWN[0]], e.o_mix.at[:, own[0]]),
+            (e.dmix.at[r, OWN[1]], e.o_mix.at[:, own[1]]),
+            (e.dmix.at[r, OWN[2]], e.o_mix.at[:, own[2]]),
+            (e.daux.at[to], e.daux_in.at[j]),
+        )[n]
         k = 2 * t + dc
-        return [
-            remote(src, dst, e.fsend.at[k, n], e.frecv.at[k, n], base + to)
-            for n, (src, dst) in enumerate(pairs)
-        ]
+        return remote(src, dst, e.fsend.at[k, n], e.frecv.at[k, n], base + to)
+
+    def target(t):
+        return lax.rem(y + CHIPS - 1 - t, CHIPS)
+
+    def read(t, carry):
+        read_pair(e, target(t))
+
+        @pl.when(t < CHIPS - 1)
+        def _():
+            token_copy(t, 0, 0).start()
+
+        token_copy(t, 1, 0).start()
+        return carry
+
+    lax.fori_loop(0, CHIPS, read, 0)
+    back.wait()
 
     def edge_copy(i, at):
         return remote(
             e.edge.at[at], e.edges.at[j], e.esend.at[at], e.erecv.at[j], base + 2 * i + 1
         )
 
+    def edge_goes(i, t):
+        return ((i == CHIPS - 1) & (j != last)) | ((t == 0) & (i < CHIPS - 1))
+
     def back_copy(i, at):
         to = jnp.where(i == 0, before + last, base + 2 * i - 1)
         return remote(e.back.at[at], e.backs.at[j], e.bsend.at[at], e.brecv.at[j], to)
 
+    def back_goes(i, t):
+        return (i == 0) | (t == CHIPS - 1)
+
     def finish(t, carry):
-        i = lax.rem(y + t + 1, CHIPS)
+        i = target(t)
         finish_pair(e, i, t, taps)
 
         @pl.when(t < CHIPS - 1)
         def _():
-            for copy in token_copies(t, 0):
-                copy.start()
-
-        for copy in token_copies(t, 1):
-            copy.start()
-
-        @pl.when(2 * i + 1 == j)
+            for n in range(1, 5):
+                token_copy(t, 0, n).start()
+
+        for n in range(1, 5):
+            token_copy(t, 1, n).start()
+
+        @pl.when(edge_goes(i, t))
+        def _():
+            edge_copy(i, t).start()
+
+        @pl.when((i == CHIPS - 1) & (j == last))
         def _():
             e.edges[j] = e.edge[t]
 
-        @pl.when(2 * i + 1 != j)
-        def _():
-            edge_copy(i, t).start()
-
-        @pl.when((i > 0) & (2 * i - 1 == j))
-        def _():
-            e.backs[j] = e.back[t]
-
-        @pl.when((i == 0) | (2 * i - 1 != j))
+        @pl.when(back_goes(i, t))
         def _():
             back_copy(i, t).start()
 
@@ -736,8 +785,8 @@
     for t in range(CHIPS):
         for dc in range(2):
             if (t, dc) != (CHIPS - 1, 0):
-                for copy in token_copies(t, dc):
-                    copy.wait()
+                for n in range(5):
+                    token_copy(t, dc, n).wait()
 
     @pl.when(c == 1)
     def _():
@@ -753,25 +802,25 @@
                     e.back.at[0], e.backs.at[src], e.bsend.at[0], e.brecv.at[src], base + last
                 )
 
-            @pl.when(j != src)
+            whole_row = y == CHIPS - 1
+
+            @pl.when(whole_row | (y + 1 == src // 2))
             def _():
-                edge_from().wait_recv()
-
-            @pl.when(jnp.logical_not(inside) | (j != src))
-            def _():
+                @pl.when(j != src)
+                def _():
+                    edge_from().wait_recv()
+
                 back_from().wait_recv()
-
-        for src in range(GROUP):
-            fixed = e.edges[src] + e.backs[src]
-            spots = (
-                (src * DK, DK, 0),
-                ((KH + src) * DK, DK, DK),
-                ((2 * KH + 2 * src) * DK, 2 * DK, 2 * DK),
-            )
-            for at, width, own_at in spots:
-                old = e.o_mix[112:128, at : at + width].astype(f32)
-                new = jnp.concatenate([old[0:8], fixed[:, own_at : own_at + width]], axis=0)
-                e.o_mix[112:128, at : at + width] = new.astype(bf16)
+                fixed = e.edges[src] + e.backs[src]
+                spots = (
+                    (src * DK, DK, 0),
+                    ((KH + src) * DK, DK, DK),
+                    ((2 * KH + 2 * src) * DK, 2 * DK, 2 * DK),
+                )
+                for at, width, own_at in spots:
+                    old = e.o_mix[112:128, at : at + width].astype(f32)
+                    new = jnp.concatenate([old[0:8], fixed[:, own_at : own_at + width]], axis=0)
+                    e.o_mix[112:128, at : at + width] = new.astype(bf16)
 
     for src in range(GROUP):
         e.o_decay[2 * src : 2 * src + 2, :] = e.daux_in[src][0:2, :]
@@ -788,13 +837,13 @@
     for n in range(1, 16):
         tap_copy(n).wait_send()
     for t in range(CHIPS):
-        i = lax.rem(y + t + 1, CHIPS)
-
-        @pl.when(2 * i + 1 != j)
+        i = target(t)
+
+        @pl.when(edge_goes(i, t))
         def _():
             edge_copy(i, t).wait_send()
 
-        @pl.when((i == 0) | (2 * i - 1 != j))
+        @pl.when(back_goes(i, t))
         def _():
             back_copy(i, t).wait_send()
 
@@ -820,10 +869,26 @@
     )(*args)
 
 
+def emit_kernel(*refs):
+    for src, dst in zip(refs[:5], refs[5:]):
+        dst[...] = src[...]
+
+
+def emit(*arrays):
+    return pl.pallas_call(
+        emit_kernel,
+        out_shape=tuple(jax.ShapeDtypeStruct(x.shape, x.dtype) for x in arrays),
+        in_specs=[vspec] * 5,
+        out_specs=(vspec,) * 5,
+        name="emit",
+    )(*arrays)
+
+
 def local(mixed, conv_weight, log_decay, beta, doc_ids, out_grad):
     out, dmix, taps, d_decay, d_beta = layer(
         mixed[0], conv_weight, log_decay[0], beta[0], doc_ids, out_grad[0]
     )
+    out, dmix, taps, d_decay, d_beta = emit(out, dmix, taps, d_decay, d_beta)
     return out[None], dmix[None], taps, d_decay[None], d_beta[None]
 
 

time: 77.1 us -> 71.1 us (0.922)
  local copies, waits for them, and re-layouts: 4.94 us -> 0 us
    unnamed x13 -> x0, local copies, waits for them, and re-layouts: 4.94 us -> none
    pallas_call x1, Pallas kernels: 70.9 us -> 67.7 us  [layer(): pl.pallas_call(layer_kernel, out_shape=(jax.ShapeDtypeStruct((128, 2 * KH...]
    pallas_call x0 -> x1, Pallas kernels: none -> 2.6 us  [emit(): pl.pallas_call(emit_kernel, out_shape=tuple((jax.ShapeDtypeStruct(x.shape...]
where the time goes in v3:
time: 71.1 us; the launch traced here: 71 us
  Pallas kernels  70.3 us (99%)
    pallas_call x1, Pallas kernels, layer(): pl.pallas_call(layer_kernel, out_shape=(jax.ShapeDtypeStruct((128, 2 * KH...  67.7 us
    pallas_call x1, Pallas kernels, emit(): pl.pallas_call(emit_kernel, out_shape=tuple((jax.ShapeDtypeStruct(x.shape...  2.6 us

profile of v3, /device:TPU:1, one launch (start us, length us, event | category | flops | bytes accessed | tf_op | source)
XLA Modules:
  0.0 71.0 jit_solution(8492636558202328439)
XLA Ops:
  0.6 67.7 %layer.1 = (bf16[128,2048]{1,0:T(8,128)(2,1)}, bf16[128,4096]{1,0:T(8,128)(2,1)}, f32[4,4096]{1,0:T(4,128)}, f32[16,128]{1,0:T(8,128)}, f32[16,128]{1,0:T(8,128)}) custom-call(bf16[128,4096]{1,0:T(8,128)(2,1)} %bitcast.8, bf16[4,4096]{1,0:T(4,128)(2,1)} %refs_1_.1, f32[16,128]{1,0:T(8,128)} %bitcast.10, f32[16,128]{1,0:T(8,128)} %bitcast.11, ...), custom_call_target="tpu_custom_call" | custom-call | tf_op jit(solution)/shard_map/layer/pallas_call | solution.py:853
  68.3 2.6 %emit.1 = (bf16[128,2048]{1,0:T(8,128)(2,1)}, bf16[128,4096]{1,0:T(8,128)(2,1)}, f32[4,4096]{1,0:T(4,128)}, f32[16,128]{1,0:T(8,128)}, f32[16,128]{1,0:T(8,128)}) custom-call(bf16[128,2048]{1,0:T(8,128)(2,1)} %get-tuple-element.15.refs_0_, bf16[128,4096]{1,0:T(8,128)(2,1)} %get-tuple-element.16.refs_1_, f32[4,4096]{1,0:T(4,128)} %get-tuple-element.17.refs_2_, ...), custom_call_target="tpu_custom_call" | custom-call | tf_op jit(solution)/shard_map/emit/pallas_call | solution.py:878

commit v4 on v3

--- a/solution.py
+++ b/solution.py
@@ -187,14 +187,13 @@
                     keep=keep,
                 )
             )
-    inverse = invert([c["low"] for c in chains])
-    for c, t in zip(chains, inverse):
+    inverse = [split(t) for t in invert([c["low"] for c in chains])]
+    lefts = [split(mm(split(c["left"]), t)) for c, t in zip(chains, inverse)]
+    bigs = [wide(stack(t, x), split(c["right"])) for c, t, x in zip(chains, inverse, lefts)]
+    for c, ns, big in zip(chains, lefts, bigs):
         n = c["n"]
-        ts = split(t)
-        ns = split(mm(split(c["left"]), ts))
         e.nh[n] = ns[0]
         e.nl[n] = ns[1]
-        big = wide(stack(ts, ns), split(c["right"]))
         ws = split(jnp.concatenate([big[:L, :DK], c["eq"] - big[L : 2 * L, :DK]], axis=0))
         e.wh[n] = ws[0]
         e.wl[n] = ws[1]
@@ -282,73 +281,79 @@
     sigma = 1.0 / (1.0 + jnp.exp(-sm))
     active = sm * sigma
     left = [split(e.arrived[2 + h]) for h in range(2)]
-    pieces = []
+
+    def dot(a, b):
+        return lax.dot_general(a, b, NT, preferred_element_type=f32)
+
+    spots = [(p, h) for p in range(PER) for h in range(2)]
+    index = [2 * (PER * i + p) + h for p, h in spots]
+    starts = [pl.multiple_of(r0 + p * L, L) for p in range(PER)]
+    later = [
+        e.rt[n + 2] + mm(left[h], split(e.ps[n + 2])) for (p, h), n in zip(spots, index)
+    ]
+    laters = [split(x) for x in later]
+    turned = [
+        mm((e.gt[n],), (e.nh[n][:L], e.nl[n][:L])) + mm(x, (e.nh[n][L:], e.nl[n][L:]))
+        for n, x in zip(index, laters)
+    ]
+    ys = [jnp.transpose(x) for x in turned]
+    us = [split(e.u[n]) for n in index]
+    states = [split(e.st[n]) for n in index]
+    grads = [e.grad[pl.ds(starts[p], L), h * DK : (h + 1) * DK] for p, h in spots]
+    tops = [jnp.concatenate((g,) + split(y), axis=0) for g, y in zip(grads, ys)]
+    rights = [stack(u, x) for u, x in zip(us, states)]
+    res = [dot(a, b[0]) for a, b in zip(tops, rights)]
+    fine = [dot(a[: 2 * L], b[1]) for a, b in zip(tops, rights)]
+    tails = [mm(u, x) for u, x in zip(us, laters)]
+    pieces, scores, lows = [], [], []
     for p in range(PER):
-        lo = slice(p * L, (p + 1) * L)
         block = PER * i + p
-        rb = pl.multiple_of(r0 + p * L, L)
+        rb = starts[p]
         tile = e.tile[block]
         columns = e.cs[8 + p * L : 8 + (p + 1) * L, :]
         doc_before = e.cs[7 + p * L : 8 + p * L, 4:5]
-        d_score = jnp.zeros((L, L), f32)
-        d_low = jnp.zeros((L, L), f32)
-        dq = jnp.zeros((L, DK), f32)
-        dk = jnp.zeros((L, DK), f32)
+        d_score = d_low = dq = dk = 0.0
         small = jnp.zeros((L, L), f32)
-        dvs, ends = [], []
+        dvs = []
         for h in range(2):
-            n = 2 * block + h
+            m = 2 * p + h
+            n = index[m]
             fade, enter, cum, cum_row, doc_row, doc_last, cum_last = gates(
                 tile, h, columns[:, 4:5], doc_before, columns
             )
             rate = columns[:, 2 + h : 3 + h]
             tail = jnp.where(columns[:, 4:5] == doc_last, jnp.exp(cum_last - cum), 0.0)
-            state = split(e.st[n])
-            later = e.rt[n + 2] + mm(left[h], split(e.ps[n + 2]))
-            laters = split(later)
-            u = e.u[n]
-            out = e.o[n]
-            g = e.grad[pl.ds(rb, L), h * DK : (h + 1) * DK]
-            ns = (e.nh[n], e.nl[n])
-            yt = mm((e.gt[n],), (ns[0][:L], ns[1][:L])) + mm(laters, (ns[0][L:], ns[1][L:]))
-            y = jnp.transpose(yt)
-            ys = split(y)
-            us = split(u)
-            right = stack(us, state)
-            tops = jnp.concatenate([g, ys[0], ys[1]], axis=0)
-
-            def dot(a, b):
-                return lax.dot_general(a, b, NT, preferred_element_type=f32)
-
-            res = dot(tops, right[0])
-            fine = dot(tops[: 2 * L], right[1])
-            gu = res[:L] + fine[:L]
-            yu = res[L : 2 * L] + res[2 * L :] + fine[L:]
+            gu = res[m][:L] + fine[m][:L]
+            yu = res[m][L : 2 * L] + res[m][2 * L :] + fine[m][L:]
             d_score = d_score + gu[:, :L] * fade
             d_low = d_low - jnp.where(ri > ci, yu[:, :L] * (rate * fade), 0.0)
             dq = dq + enter * gu[:, L:]
-            dk = dk - (enter * rate) * yu[:, L:]
-            dv = rate * y
+            dk = dk + tail * tails[m] - (enter * rate) * yu[:, L:]
+            dv = rate * ys[m]
             dvs.append(dv)
-            ends.append((us, tail, laters))
-            v = active[lo, (2 + h) * DK : (3 + h) * DK]
-            d_cum = jnp.sum(out * g.astype(f32) - v * dv, -1, keepdims=True)
-            end = jnp.sum(e.st[n + 2] * jnp.transpose(later), -1, keepdims=True)
+            v = active[p * L : (p + 1) * L, (2 + h) * DK : (3 + h) * DK]
+            d_cum = jnp.sum(e.o[n] * grads[m].astype(f32) - v * dv, -1, keepdims=True)
+            end = jnp.sum(e.st[n + 2] * jnp.transpose(later[m]), -1, keepdims=True)
             end = jnp.sum(end, 0, keepdims=True)
             d_cum = d_cum + jnp.where(ri[:, 0:1] == L - 1, end, 0.0)
-            d_rate = jnp.sum(y * u, -1, keepdims=True) / rate
+            d_rate = jnp.sum(ys[m] * e.u[n], -1, keepdims=True) / rate
             small = small + jnp.where(ci == h, d_cum, 0.0) + jnp.where(ci == 2 + h, d_rate, 0.0)
-        ks = split(e.k[pl.ds(rb, L), :])
-        qs = split(e.q[pl.ds(rb, L), :])
-        both = mm(split(jnp.concatenate([d_score, d_low + jnp.transpose(d_low)], axis=0)), ks)
-        dq = dq + both[:L]
-        dk = dk + both[L:] + mm(split(jnp.transpose(d_score)), qs)
-        for us, tail, laters in ends:
-            dk = dk + tail * mm(us, laters)
-        small = jnp.transpose(small)[0:8, :]
-        which = lax.broadcasted_iota(jnp.int32, (8, 128), 0)
-        e.daux[block] = jnp.where(which < 2, exact(small, lower), small)
-        pieces.append((dq, dk, dvs[0], dvs[1]))
+        scores.append(d_score)
+        lows.append(d_low)
+        pieces.append([dq, dk, dvs[0], dvs[1], small])
+    ks = [split(e.k[pl.ds(x, L), :]) for x in starts]
+    qs = [split(e.q[pl.ds(x, L), :]) for x in starts]
+    firsts = [
+        split(jnp.concatenate([x, y + jnp.transpose(y)], axis=0)) for x, y in zip(scores, lows)
+    ]
+    firsts = [mm(x, k) for x, k in zip(firsts, ks)]
+    seconds = [mm(split(jnp.transpose(x)), q) for x, q in zip(scores, qs)]
+    which = lax.broadcasted_iota(jnp.int32, (8, 128), 0)
+    for p in range(PER):
+        pieces[p][0] = pieces[p][0] + firsts[p][:L]
+        pieces[p][1] = pieces[p][1] + firsts[p][L:] + seconds[p]
+        small = jnp.transpose(pieces[p].pop())[0:8, :]
+        e.daux[PER * i + p] = jnp.where(which < 2, exact(small, lower), small)
     dq, dk, dv0, dv1 = (jnp.concatenate(x, axis=0) for x in zip(*pieces))
     aq, ak = active[:, :DK], active[:, DK : 2 * DK]
     nq = lax.rsqrt(jnp.sum(aq * aq, -1, keepdims=True) + EPS)
@@ -869,17 +874,35 @@
     )(*args)
 
 
+HALVES = ((0, 0, 128), (1, 0, 64), (1, 64, 64), (2, 0, 4), (3, 0, 16), (4, 0, 16))
+
+
 def emit_kernel(*refs):
-    for src, dst in zip(refs[:5], refs[5:]):
-        dst[...] = src[...]
+    srcs, dsts, mids, (come, go) = refs[:5], refs[5:10], refs[10:15], refs[15:]
+    into, out = [], []
+    for n, (a, r, size) in enumerate(HALVES):
+        rows = pl.ds(r, size)
+        mid = mids[a].at[rows]
+        into.append(pltpu.make_async_copy(srcs[a].at[rows], mid, come.at[n]))
+        out.append(pltpu.make_async_copy(mid, dsts[a].at[rows], go.at[n]))
+    for copy in into:
+        copy.start()
+    for first, second in zip(into, out):
+        first.wait()
+        second.start()
+    for copy in out:
+        copy.wait()
 
 
 def emit(*arrays):
+    far = pl.BlockSpec(memory_space=pl.ANY)
+    sems = pltpu.SemaphoreType.DMA((len(HALVES),))
     return pl.pallas_call(
         emit_kernel,
         out_shape=tuple(jax.ShapeDtypeStruct(x.shape, x.dtype) for x in arrays),
-        in_specs=[vspec] * 5,
-        out_specs=(vspec,) * 5,
+        in_specs=[far] * 5,
+        out_specs=(far,) * 5,
+        scratch_shapes=[VM(x.shape, x.dtype) for x in arrays] + [sems, sems],
         name="emit",
     )(*arrays)
 

time: 71.1 us -> 70 us (0.985)
  Pallas kernels: 70.3 us -> 69.2 us
    pallas_call x1, Pallas kernels: 67.7 us -> 66.9 us  [layer(): pl.pallas_call(layer_kernel, out_shape=(jax.ShapeDtypeStruct((128, 2 * KH...]
where the time goes in v4:
time: 70 us; the launch traced here: 69.8 us
  Pallas kernels  69.2 us (99%)
    pallas_call x1, Pallas kernels, layer(): pl.pallas_call(layer_kernel, out_shape=(jax.ShapeDtypeStruct((128, 2 * KH...  66.9 us
    pallas_call x1, Pallas kernels, emit(): pl.pallas_call(emit_kernel, out_shape=tuple((jax.ShapeDtypeStruct(x.shape...  2.3 us

profile of v4, /device:TPU:1, one launch (start us, length us, event | category | flops | bytes accessed | tf_op | source)
XLA Modules:
  0.0 69.8 jit_solution(16876206273712134562)
XLA Ops:
  0.6 66.9 %layer.1 = (bf16[128,2048]{1,0:T(8,128)(2,1)}, bf16[128,4096]{1,0:T(8,128)(2,1)}, f32[4,4096]{1,0:T(4,128)}, f32[16,128]{1,0:T(8,128)}, f32[16,128]{1,0:T(8,128)}) custom-call(bf16[128,4096]{1,0:T(8,128)(2,1)} %bitcast.8, bf16[4,4096]{1,0:T(4,128)(2,1)} %refs_1_.1, f32[16,128]{1,0:T(8,128)} %bitcast.10, f32[16,128]{1,0:T(8,128)} %bitcast.11, ...), custom_call_target="tpu_custom_call" | custom-call | tf_op jit(solution)/shard_map/layer/pallas_call | solution.py:858
  67.5 2.3 %emit.1 = (bf16[128,2048]{1,0:T(8,128)(2,1)}, bf16[128,4096]{1,0:T(8,128)(2,1)}, f32[4,4096]{1,0:T(4,128)}, f32[16,128]{1,0:T(8,128)}, f32[16,128]{1,0:T(8,128)}) custom-call(bf16[128,2048]{1,0:T(8,128)(2,1)} %get-tuple-element.15.refs_0_, bf16[128,4096]{1,0:T(8,128)(2,1)} %get-tuple-element.16.refs_1_, f32[4,4096]{1,0:T(4,128)} %get-tuple-element.17.refs_2_, ...), custom_call_target="tpu_custom_call" | custom-call | tf_op jit(solution)/shard_map/emit/pallas_call | solution.py:900

commit v5 on v4

--- a/solution.py
+++ b/solution.py
@@ -206,14 +206,15 @@
 
 
 def backward_terms(e, i):
-    for p in range(PER):
-        rb = pl.multiple_of(i * ROWS + p * L, L)
-        for h in range(2):
-            n = (PER * i + p) * 2 + h
-            g = e.grad[pl.ds(rb, L), h * DK : (h + 1) * DK]
-            turned = jnp.transpose(g.astype(f32)).astype(bf16)
-            e.gt[n] = turned
-            e.r[n] = mm((turned,), (e.wh[n][L:], e.wl[n][L:]))
+    spots = [(p, h) for p in range(PER) for h in range(2)]
+    index = [2 * (PER * i + p) + h for p, h in spots]
+    starts = [pl.multiple_of(i * ROWS + p * L, L) for p in range(PER)]
+    grads = [e.grad[pl.ds(starts[p], L), h * DK : (h + 1) * DK] for p, h in spots]
+    turned = [jnp.transpose(g.astype(f32)).astype(bf16) for g in grads]
+    terms = [mm((g,), (e.wh[n][L:], e.wl[n][L:])) for n, g in zip(index, turned)]
+    for n, g, r in zip(index, turned, terms):
+        e.gt[n] = g
+        e.r[n] = r
 
 
 def scan_forward(e):
@@ -259,17 +260,19 @@
 
 def read_pair(e, i):
     entered = [split(e.arrived[h]) for h in range(2)]
-    for p in range(PER):
+    spots = [(p, h) for p in range(PER) for h in range(2)]
+    index = [2 * (PER * i + p) + h for p, h in spots]
+    states = [
+        e.st[n] + mm(split(e.pi[n]), entered[h]) for n, (p, h) in zip(index, spots)
+    ]
+    both = [mm((e.wh[n], e.wl[n]), split(x)) for n, x in zip(index, states)]
+    for n, (p, h), state, x in zip(index, spots, states, both):
         rb = pl.multiple_of(i * ROWS + p * L, L)
-        for h in range(2):
-            n = 2 * (PER * i + p) + h
-            state = e.st[n] + mm(split(e.pi[n]), entered[h])
-            e.st[n] = state
-            both = mm((e.wh[n], e.wl[n]), split(state))
-            e.u[n] = e.u[n] - both[:L]
-            out = e.o[n] + both[L:]
-            e.o[n] = out
-            e.out[pl.ds(rb, L), h * DK : (h + 1) * DK] = out.astype(bf16)
+        e.st[n] = state
+        e.u[n] = e.u[n] - x[:L]
+        out = e.o[n] + x[L:]
+        e.o[n] = out
+        e.out[pl.ds(rb, L), h * DK : (h + 1) * DK] = out.astype(bf16)
 
 
 def finish_pair(e, i, t, taps):

time: 70 us -> 69.8 us (level)
  no operation moved by 1% of the time
where the time goes in v5:
time: 69.8 us; the launch traced here: 69.7 us
  Pallas kernels  69 us (99%)
    pallas_call x1, Pallas kernels, layer(): pl.pallas_call(layer_kernel, out_shape=(jax.ShapeDtypeStruct((128, 2 * KH...  66.7 us
    pallas_call x1, Pallas kernels, emit(): pl.pallas_call(emit_kernel, out_shape=tuple((jax.ShapeDtypeStruct(x.shape...  2.3 us

profile of v5, /device:TPU:1, one launch (start us, length us, event | category | flops | bytes accessed | tf_op | source)
XLA Modules:
  0.0 69.7 jit_solution(1184474027109254010)
XLA Ops:
  0.6 66.7 %layer.1 = (bf16[128,2048]{1,0:T(8,128)(2,1)}, bf16[128,4096]{1,0:T(8,128)(2,1)}, f32[4,4096]{1,0:T(4,128)}, f32[16,128]{1,0:T(8,128)}, f32[16,128]{1,0:T(8,128)}) custom-call(bf16[128,4096]{1,0:T(8,128)(2,1)} %bitcast.8, bf16[4,4096]{1,0:T(4,128)(2,1)} %refs_1_.1, f32[16,128]{1,0:T(8,128)} %bitcast.10, f32[16,128]{1,0:T(8,128)} %bitcast.11, ...), custom_call_target="tpu_custom_call" | custom-call | tf_op jit(solution)/shard_map/layer/pallas_call | solution.py:861
  67.4 2.3 %emit.1 = (bf16[128,2048]{1,0:T(8,128)(2,1)}, bf16[128,4096]{1,0:T(8,128)(2,1)}, f32[4,4096]{1,0:T(4,128)}, f32[16,128]{1,0:T(8,128)}, f32[16,128]{1,0:T(8,128)}) custom-call(bf16[128,2048]{1,0:T(8,128)(2,1)} %get-tuple-element.15.refs_0_, bf16[128,4096]{1,0:T(8,128)(2,1)} %get-tuple-element.16.refs_1_, f32[4,4096]{1,0:T(4,128)} %get-tuple-element.17.refs_2_, ...), custom_call_target="tpu_custom_call" | custom-call | tf_op jit(solution)/shard_map/emit/pallas_call | solution.py:903
